TPU v7x, 512 devices: a whole 4x8x8 slice. The times are simulated.
512 devices in a mesh: px: 16 (over z, core), py: 32 (over x, y).
Axes of the slice: x: 4, y: 8, z: 8, core: 2. Of those that a mesh axis runs over, the one named last changes fastest.
Arguments:
- field_in: bfloat16 [32, 32, 512, 512], P(None, 'py', 'px'), may hold values from -6 to 6
- cotangent: bfloat16 [32, 32, 512, 512], P(None, 'py', 'px'), may hold values from -6 to 6
- spectrum_saved: float32 [32, 32, 32, 32, 2], P(None, None, 'px', 'py'), may hold values from -6 to 6
- weight_store: float32 [2048, 2, 32, 32], P(('px', 'py')), may hold values from -4.2 to 4.2
- block_slot: int32 [32, 32], P('py', 'px'), may hold values from 0 to 127, as said below
- kx_modes: int32 [32], replicated, may hold values from 0 to 511, as said below
- ky_modes: int32 [32], replicated, may hold values from 0 to 511, as said below
- pointwise: bfloat16 [32, 32], replicated, may hold values from -0.25 to 0.25
- bias_vector: float32 [32], replicated, may hold values from -3 to 3
Outputs:
- field_grad: float32 [32, 32, 512, 512], P(None, 'py', 'px')
- store_grad: float32 [2048, 2, 32, 32], P(('px', 'py'))
Inputs may be any that keep to these rules, and one draw needn't show every extreme that they name: `kx_modes`: 32 distinct wave numbers k, each with k < 32 or k > 480. `ky_modes`: 32 distinct wave numbers k, each with k < 32 or k > 480. `block_slot`: within each px index's 2 second-dimension modes, the values over all 32 x 2 mode pairs are distinct; v // 4 is the py index of the device that stores the block and v % 4 its slot there; in each such group one py index stores 4 blocks, and the other slots hold unused blocks.
All inputs are finite; a program needn't handle non-finite values.
Results may differ from a plain program's by a relative error of at most 0.0003.
Values sent between devices are 32-bit elements; how exact they have to be, the bound alone decides.
A program may use at most 64 MiB of HBM per device.

v0:
```python
import math

import jax
import jax.numpy as jnp
from jax import lax
from jax.sharding import PartitionSpec as P

precise = lax.Precision.HIGHEST


def phase_table(length, modes):
    points = lax.iota(jnp.int32, length)
    wrapped = points[:, None] * modes[None, :] % length
    angle = wrapped.astype(jnp.float32) * (2.0 * math.pi / length)
    return (jnp.cos(angle), jnp.sin(angle))


def gelu_slope(values):
    normal_cdf = 0.5 * (1.0 + lax.erf(values * 0.7071067811865476))
    density = jnp.exp(-0.5 * values * values) * 0.3989422804014327
    return normal_cdf + values * density


def channel_mix(blocks, spectrum):
    block_re = blocks[:, :, 0]
    block_im = blocks[:, :, 1]
    spec_re = spectrum[..., 0]
    spec_im = spectrum[..., 1]
    form = "baoc,czba->ozba"
    out_re = jnp.einsum(form, block_re, spec_re, precision=precise) - jnp.einsum(
        form, block_im, spec_im, precision=precise
    )
    out_im = jnp.einsum(form, block_re, spec_im, precision=precise) + jnp.einsum(
        form, block_im, spec_re, precision=precise
    )
    return jnp.stack([out_re, out_im], -1)


def channel_adjoint(blocks, spectrum):
    block_re = blocks[:, :, 0]
    block_im = blocks[:, :, 1]
    grad_re = spectrum[..., 0]
    grad_im = spectrum[..., 1]
    form = "baoc,ozba->czba"
    out_re = jnp.einsum(form, block_re, grad_re, precision=precise) + jnp.einsum(
        form, block_im, grad_im, precision=precise
    )
    out_im = jnp.einsum(form, block_re, grad_im, precision=precise) - jnp.einsum(
        form, block_im, grad_re, precision=precise
    )
    return jnp.stack([out_re, out_im], -1)


def block_gradient(spectrum_grad, spectrum):
    grad_re = spectrum_grad[..., 0]
    grad_im = spectrum_grad[..., 1]
    spec_re = spectrum[..., 0]
    spec_im = spectrum[..., 1]
    form = "ozba,czba->aboc"
    out_re = jnp.einsum(form, grad_re, spec_re, precision=precise) + jnp.einsum(
        form, grad_im, spec_im, precision=precise
    )
    out_im = jnp.einsum(form, grad_im, spec_re, precision=precise) - jnp.einsum(
        form, grad_re, spec_im, precision=precise
    )
    return jnp.stack([out_re, out_im], 2)


def invert_rows(spectrum, cos_rows, sin_rows):
    spec_re = spectrum[..., 0]
    spec_im = spectrum[..., 1]
    form = "czma,xa->czmx"
    back_re = jnp.einsum(form, spec_re, cos_rows, precision=precise) - jnp.einsum(
        form, spec_im, sin_rows, precision=precise
    )
    back_im = jnp.einsum(form, spec_re, sin_rows, precision=precise) + jnp.einsum(
        form, spec_im, cos_rows, precision=precise
    )
    joined = jnp.stack([back_re, back_im], 3)
    return joined.reshape(joined.shape[0], joined.shape[1], 2 * joined.shape[2], joined.shape[4])


def on_device(
    field_in,
    cotangent,
    spectrum_saved,
    weight_store,
    block_slot,
    kx_modes,
    ky_modes,
    pointwise,
    bias_vector,
):
    channels, planes, rows_x, width_y = field_in.shape
    full_x = rows_x * lax.axis_size("px")
    modes_y = ky_modes.shape[0]
    local_y = modes_y // lax.axis_size("px")
    capacity = weight_store.shape[0]
    factor = 1.0 / math.sqrt(full_x * width_y)
    cos_y, sin_y = phase_table(width_y, ky_modes)
    table_y = jnp.stack([cos_y, -sin_y], 2).reshape(width_y, 2 * modes_y)
    cos_x, sin_x = phase_table(full_x, kx_modes)
    store_row, slots_row = (
        lax.all_gather(weight_store, "py", axis=0, tiled=True),
        lax.all_gather(block_slot, "py", axis=0, tiled=True),
    )
    slots_flat = slots_row.reshape(-1)

    def inverse_planes(spectrum):
        joined = invert_rows(spectrum, cos_x, sin_x)
        returned = lax.all_to_all(joined, "px", split_axis=3, concat_axis=2, tiled=True)
        return factor * jnp.einsum("czkx,yk->czxy", returned, table_y, precision=precise)

    weight_full = pointwise.astype(jnp.float32)
    local_x = block_slot.shape[0]
    indices = jnp.transpose(block_slot).reshape(-1)
    blocks = jnp.take(store_row, indices, axis=0).reshape(local_y, local_x, 2, channels, channels)
    mixed = channel_mix(blocks, spectrum_saved)

    def from_modes(spectrum):
        return lax.all_to_all(spectrum, "py", split_axis=1, concat_axis=3, tiled=True)

    spectral = inverse_planes(from_modes(mixed))
    mapped = jnp.einsum("oc,czxy->ozxy", pointwise, field_in, preferred_element_type=jnp.float32)
    grad = cotangent.astype(jnp.float32) * gelu_slope(
        mapped + bias_vector.reshape(channels, 1, 1, 1) + spectral
    )
    partial_value = jnp.einsum("czxy,yk->czkx", grad, table_y, precision=precise)
    moved = lax.all_to_all(partial_value, "px", split_axis=2, concat_axis=3, tiled=True)
    pieces = moved.reshape(channels, planes, local_y, 2, full_x)
    part_re = pieces[:, :, :, 0]
    part_im = pieces[:, :, :, 1]
    form = "czmx,xk->czmk"
    real_part = jnp.einsum(form, part_re, cos_x, precision=precise) + jnp.einsum(
        form, part_im, sin_x, precision=precise
    )
    imag_part = jnp.einsum(form, part_im, cos_x, precision=precise) - jnp.einsum(
        form, part_re, sin_x, precision=precise
    )
    spectrum_grad = lax.all_to_all(
        factor * jnp.stack([real_part, imag_part], -1),
        "py",
        split_axis=3,
        concat_axis=1,
        tiled=True,
    )
    input_spectrum = channel_adjoint(blocks, spectrum_grad)
    local_grad = block_gradient(spectrum_grad, spectrum_saved)
    field_grad = jnp.einsum("oc,ozxy->czxy", weight_full, grad, precision=precise) + inverse_planes(
        from_modes(input_spectrum)
    )
    grads_all = lax.all_gather(local_grad, "py", axis=0, tiled=True)
    grads_flat = grads_all.reshape(slots_flat.shape[0], 2 * channels * channels)
    targets = lax.axis_index("py") * capacity + lax.iota(jnp.int32, capacity)
    select = (targets[:, None] == slots_flat[None, :]).astype(jnp.float32)
    store_flat = jnp.dot(select, grads_flat, precision=precise)
    store_grad = store_flat.reshape(capacity, 2, channels, channels)
    return (field_grad, store_grad)


def solution(mesh):
    placed = (
        P(None, "py", "px", None),
        P(None, "py", "px", None),
        P(None, None, "px", "py", None),
        P(("px", "py"), None, None, None),
        P("py", "px"),
        P(),
        P(),
        P(),
        P(),
    )
    return jax.shard_map(
        on_device,
        mesh=mesh,
        in_specs=placed,
        out_specs=(P(None, "py", "px", None), P(("px", "py"), None, None, None)),
        check_vma=False,
    )
```

profile of v0, /device:TPU:64, one launch (start us, length us, event | category | flops | bytes accessed | tf_op | source)
XLA Modules:
  0.0 343.6 jit_solution(8667537079059800114)
XLA Ops:
  10.2 91.8 %all-gather.3.cloned.1.call-done = f32[128,2,32,32]{3,2,1,0:T(8,128)} async-done(((f32[4,2,32,32]{3,2,1,0:T(8,128)}), f32[128,2,32,32]{3,2,1,0:T(8,128)}) %all-gather.3.cloned.1.call-update) | async-done | bytes 1048592 | tf_op jit(solution)/shard_map/all_gather | solution.py:104
  102.0 2.7 gather_fusion
  105.8 15.5 %all_to_all.99 = f32[32,1,128]{2,1,0:T(1,128)S(1)} all-to-all(f32[32,1,128]{2,1,0:T(1,128)S(1)} %reshape.429), channel_id=1, replica_groups=mesh['px'=16,'py'=32] {'py'}, dimensions={0} | all-to-all | bytes 32768 | tf_op jit(solution)/shard_map/all_to_all | solution.py:121
  128.2 7.8 %all-to-all-start.1 = ((f32[16,1,4096]{2,1,0:T(1,128)}), f32[16,1,4096]{2,1,0:T(1,128)S(1)}, u32[]{:S(2)}, u32[]{:S(2)}) async-start(f32[16,1,4096]{2,1,0:T(1,128)} %reshape.431), calls=%async_computation.1 | async-start | bytes 524288 | tf_op jit(solution)/shard_map/all_to_all | solution.py:111
  138.8 6.8 %all-to-all-done.1 = f32[16,1,4096]{2,1,0:T(1,128)S(1)} async-done(((f32[16,1,4096]{2,1,0:T(1,128)}), f32[16,1,4096]{2,1,0:T(1,128)S(1)}, u32[]{:S(2)}, u32[]{:S(2)}) %all-to-all-start.1) | async-done | bytes 262176 | tf_op jit(solution)/shard_map/all_to_all | solution.py:111
  149.2 6.6 %fusion.6 = f32[32,32,512]{2,0,1:T(8,128)S(1)} fusion(f32[32,32,512]{2,0,1:T(8,128)} %fusion.25, f32[32,64,32]{1,0,2:T(8,128)S(1)} %copy.172, f32[512,64,1]{0,1,2:T(8,128)S(1)} %reshape.416, bf16[32,1,32,512]{3,2,1,0:T(8,128)(2,1)} %param.10, f32[32]{0:T(128)S(1)} %copy-done.5), kind=kOutput, calls=%fused_computation.8 | convolution fusion | flops 409468928 | bytes 5636224 | tf_op jit(solution)/shard_map/czkx,yk->czxy/dot_general | solution.py:112
  157.1 2.6 fusion.10
  161.8 5.0 %all-to-all-start.2 = ((f32[16,1,4096]{2,1,0:T(1,128)}), f32[16,1,4096]{2,1,0:T(1,128)S(1)}, u32[]{:S(2)}, u32[]{:S(2)}) async-start(f32[16,1,4096]{2,1,0:T(1,128)} %reshape.433), calls=%async_computation.2 | async-start | bytes 524288 | tf_op jit(solution)/shard_map/all_to_all | solution.py:129
  166.8 33.0 %all-gather = s32[32,1,2]{2,1,0:T(1,128)S(1)} all-gather(s32[1,1,2]{2,1,0:T(1,128)S(1)} %bitcast.269), channel_id=1, replica_groups=mesh['px'=16,'py'=32] {'py'}, dimensions={0}, use_global_device_ids=true | all-gather | bytes 264 | tf_op jit(solution)/shard_map/all_gather | solution.py:105
  206.9 4.9 %all-to-all-start.3 = ((f32[32,1,128]{2,1,0:T(1,128)}), f32[32,1,128]{2,1,0:T(1,128)S(1)}, u32[]{:S(2)}, u32[]{:S(2)}) async-start(f32[32,1,128]{2,1,0:T(1,128)} %reshape.435), calls=%async_computation.3 | async-start | bytes 32768 | tf_op jit(solution)/shard_map/all_to_all | solution.py:140
  211.9 2.9 fusion.78
  214.8 6.8 %all-to-all-done.3 = f32[32,1,128]{2,1,0:T(1,128)S(1)} async-done(((f32[32,1,128]{2,1,0:T(1,128)}), f32[32,1,128]{2,1,0:T(1,128)S(1)}, u32[]{:S(2)}, u32[]{:S(2)}) %all-to-all-start.3) | async-done | bytes 16416 | tf_op jit(solution)/shard_map/all_to_all | solution.py:140
  224.7 3.8 %all-to-all-start.4 = ((f32[32,1,128]{2,1,0:T(1,128)}), f32[32,1,128]{2,1,0:T(1,128)S(1)}, u32[]{:S(2)}, u32[]{:S(2)}) async-start(f32[32,1,128]{2,1,0:T(1,128)} %reshape.437), calls=%async_computation.4 | async-start | bytes 32768 | tf_op jit(solution)/shard_map/all_to_all | solution.py:121
  228.8 9.5 %all-to-all-done.4 = f32[32,1,128]{2,1,0:T(1,128)S(1)} async-done(((f32[32,1,128]{2,1,0:T(1,128)}), f32[32,1,128]{2,1,0:T(1,128)S(1)}, u32[]{:S(2)}, u32[]{:S(2)}) %all-to-all-start.4) | async-done | bytes 16416 | tf_op jit(solution)/shard_map/all_to_all | solution.py:121
  244.4 2.6 reshape.439
  247.0 7.3 %all-to-all-start.5 = ((f32[16,1,4096]{2,1,0:T(1,128)}), f32[16,1,4096]{2,1,0:T(1,128)}, u32[]{:S(2)}, u32[]{:S(2)}) async-start(f32[16,1,4096]{2,1,0:T(1,128)} %reshape.439), calls=%async_computation.5 | async-start | bytes 524288 | tf_op jit(solution)/shard_map/all_to_all | solution.py:111
  254.3 54.2 %all_gather.11 = f32[32,2,2,32,32]{4,3,2,1,0:T(8,128)} all-gather(f32[1,2,2,32,32]{4,3,2,1,0:T(8,128)S(1)} %copy.168), channel_id=1, replica_groups=mesh['px'=16,'py'=32] {'py'}, dimensions={0}, use_global_device_ids=true | all-gather | bytes 540672 | tf_op jit(solution)/shard_map/all_gather | solution.py:152
  308.5 3.1 reshape.401
  314.0 3.4 fusion.81
  318.0 3.0 reduce.9
  323.4 2.6 copy.185
  328.6 2.7 copy.175
  331.2 2.9 fusion.7
  334.2 2.5 copy.170
  (99 shorter events, 44.9 us)
Async XLA Ops:
  7.2 129.4 %copy-start = (bf16[32,1,32,512]{3,2,1,0:T(8,128)(2,1)S(1)}, bf16[32,1,32,512]{3,2,1,0:T(8,128)(2,1)}, u32[]{:S(2)}) copy-start(bf16[32,1,32,512]{3,2,1,0:T(8,128)(2,1)} %param.9) | copy-start | bytes 3145732
  7.2 118.1 %copy-start.6 = (s32[32]{0:T(128)S(1)}, s32[32]{0:T(128)}, u32[]{:S(2)}) copy-start(s32[32]{0:T(128)} %param.14) | copy-start | bytes 388
  7.2 94.9 %all-gather.3.cloned.1.call-start = ((), (), s32[]{:S(2)}) async-start(), calls=%async_computation.6 | async-start | bytes 4325376 | tf_op jit(solution)/shard_map/all_gather | solution.py:104
  126.4 9.6 %copy-start.3 = (s32[32]{0:T(128)S(1)}, s32[32]{0:T(128)}, u32[]{:S(2)}) copy-start(s32[32]{0:T(128)} %param.15) | copy-start | bytes 388
  126.5 10.1 %copy-start.2 = (bf16[32,32]{1,0:T(8,128)(2,1)S(1)}, bf16[32,32]{1,0:T(8,128)(2,1)}, u32[]{:S(2)}) copy-start(bf16[32,32]{1,0:T(8,128)(2,1)} %param.16) | copy-start | bytes 6148
  128.2 17.4 %all-to-all-start.1 = ((f32[16,1,4096]{2,1,0:T(1,128)}), f32[16,1,4096]{2,1,0:T(1,128)S(1)}, u32[]{:S(2)}, u32[]{:S(2)}) async-start(f32[16,1,4096]{2,1,0:T(1,128)} %reshape.431), calls=%async_computation.1 | async-start | bytes 524288 | tf_op jit(solution)/shard_map/all_to_all | solution.py:111
  148.0 1.1 copy-start.5
  155.8 1.3 copy-start.1
  159.7 7.1 %copy-start.4 = (s32[1,2]{1,0:T(1,128)S(1)}, s32[1,2]{1,0:T(1,128)}, u32[]{:S(2)}) copy-start(s32[1,2]{1,0:T(1,128)} %param.13) | copy-start | bytes 28
  161.8 39.2 %all-to-all-start.2 = ((f32[16,1,4096]{2,1,0:T(1,128)}), f32[16,1,4096]{2,1,0:T(1,128)S(1)}, u32[]{:S(2)}, u32[]{:S(2)}) async-start(f32[16,1,4096]{2,1,0:T(1,128)} %reshape.433), calls=%async_computation.2 | async-start | bytes 524288 | tf_op jit(solution)/shard_map/all_to_all | solution.py:129
  206.9 14.7 %all-to-all-start.3 = ((f32[32,1,128]{2,1,0:T(1,128)}), f32[32,1,128]{2,1,0:T(1,128)S(1)}, u32[]{:S(2)}, u32[]{:S(2)}) async-start(f32[32,1,128]{2,1,0:T(1,128)} %reshape.435), calls=%async_computation.3 | async-start | bytes 32768 | tf_op jit(solution)/shard_map/all_to_all | solution.py:140
  224.7 13.6 %all-to-all-start.4 = ((f32[32,1,128]{2,1,0:T(1,128)}), f32[32,1,128]{2,1,0:T(1,128)S(1)}, u32[]{:S(2)}, u32[]{:S(2)}) async-start(f32[32,1,128]{2,1,0:T(1,128)} %reshape.437), calls=%async_computation.4 | async-start | bytes 32768 | tf_op jit(solution)/shard_map/all_to_all | solution.py:121
  247.0 71.0 %all-to-all-start.5 = ((f32[16,1,4096]{2,1,0:T(1,128)}), f32[16,1,4096]{2,1,0:T(1,128)}, u32[]{:S(2)}, u32[]{:S(2)}) async-start(f32[16,1,4096]{2,1,0:T(1,128)} %reshape.439), calls=%async_computation.5 | async-start | bytes 524288 | tf_op jit(solution)/shard_map/all_to_all | solution.py:111
Sparse Core Ops, SparseCore 0:
  11.2 90.8 all-gather.2
where the time goes:
time: 345 us; the launch traced here: 344 us
  waiting for transfers between devices  116 us (34%)
  blocking collectives  103 us (30%)
  local copies, waits for them, and re-layouts  40.7 us (12%)
  matrix products  30.9 us (9%)
  starting transfers between devices  28.8 us (8%)
  between operations  14.6 us (4%)
  other arithmetic  10.3 us (3%)
    all_gather x1, waiting for transfers between devices, on_device(): lax.all_gather(weight_store, 'py', axis=0, tiled=True)  91.8 us
    all_gather x1, blocking collectives, on_device(): grads_all = lax.all_gather(local_grad, 'py', axis=0, tiled=True)  54.2 us
    all_gather x1, blocking collectives, on_device(): lax.all_gather(block_slot, 'py', axis=0, tiled=True)  33 us
    all_to_all x1, blocking collectives, from_modes(): lax.all_to_all(spectrum, 'py', split_axis=1, concat_axis=3, tiled=True)  15.5 us
    all_to_all x2, starting transfers between devices, inverse_planes(): lax.all_to_all(joined, 'px', split_axis=3, concat_axis=2, tiled=True)  15 us
    unnamed x28, local copies, waits for them, and re-layouts  14.9 us
    dot_general x2, matrix products, inverse_planes(): jnp.einsum('czkx,yk->czxy', returned, table_y, precision=precise)  9.54 us
    all_to_all x1, waiting for transfers between devices, from_modes(): lax.all_to_all(spectrum, 'py', split_axis=1, concat_axis=3, tiled=True)  9.47 us
  transfers between devices with their start and end apart: 6, of which 4 were waited for; matrix products, arithmetic and copies ran while one was open for 6% of the time, Pallas kernels for 0%

commit v1 on v0

--- a/solution.py
+++ b/solution.py
@@ -100,11 +100,22 @@
     cos_y, sin_y = phase_table(width_y, ky_modes)
     table_y = jnp.stack([cos_y, -sin_y], 2).reshape(width_y, 2 * modes_y)
     cos_x, sin_x = phase_table(full_x, kx_modes)
-    store_row, slots_row = (
-        lax.all_gather(weight_store, "py", axis=0, tiled=True),
-        lax.all_gather(block_slot, "py", axis=0, tiled=True),
+    count_py = lax.axis_size("py")
+    wide = 2 * channels
+    pieces_out = jnp.transpose(weight_store, (2, 0, 1, 3)).reshape(channels, capacity * wide)
+    slots_out = jnp.broadcast_to(
+        block_slot.astype(jnp.float32).reshape(1, local_y), (count_py, local_y)
     )
-    slots_flat = slots_row.reshape(-1)
+    arrived = lax.all_to_all(
+        jnp.concatenate([pieces_out, slots_out], 1), "py", split_axis=0, concat_axis=0, tiled=True
+    )
+    pieces_row = arrived[:, : capacity * wide].reshape(count_py * capacity, wide)
+    slots_flat = arrived[:, capacity * wide :].reshape(-1).astype(jnp.int32)
+    select = (
+        slots_flat[:, None] == lax.iota(jnp.int32, count_py * capacity)[None, :]
+    ).astype(jnp.float32)
+    chosen = jnp.dot(select, pieces_row, precision=precise).reshape(count_py, local_y * wide)
+    rows_mine = lax.all_to_all(chosen, "py", split_axis=0, concat_axis=0, tiled=True)
 
     def inverse_planes(spectrum):
         joined = invert_rows(spectrum, cos_x, sin_x)
@@ -112,9 +123,9 @@
         return factor * jnp.einsum("czkx,yk->czxy", returned, table_y, precision=precise)
 
     weight_full = pointwise.astype(jnp.float32)
-    local_x = block_slot.shape[0]
-    indices = jnp.transpose(block_slot).reshape(-1)
-    blocks = jnp.take(store_row, indices, axis=0).reshape(local_y, local_x, 2, channels, channels)
+    blocks = jnp.transpose(
+        rows_mine.reshape(channels, local_y, 1, 2, channels), (1, 2, 3, 0, 4)
+    )
     mixed = channel_mix(blocks, spectrum_saved)
 
     def from_modes(spectrum):
@@ -149,12 +160,15 @@
     field_grad = jnp.einsum("oc,ozxy->czxy", weight_full, grad, precision=precise) + inverse_planes(
         from_modes(input_spectrum)
     )
-    grads_all = lax.all_gather(local_grad, "py", axis=0, tiled=True)
-    grads_flat = grads_all.reshape(slots_flat.shape[0], 2 * channels * channels)
-    targets = lax.axis_index("py") * capacity + lax.iota(jnp.int32, capacity)
-    select = (targets[:, None] == slots_flat[None, :]).astype(jnp.float32)
-    store_flat = jnp.dot(select, grads_flat, precision=precise)
-    store_grad = store_flat.reshape(capacity, 2, channels, channels)
+    grads_out = jnp.transpose(local_grad[0], (2, 0, 1, 3)).reshape(channels, local_y * wide)
+    grads_row = lax.all_to_all(grads_out, "py", split_axis=0, concat_axis=0, tiled=True)
+    placed = jnp.dot(
+        select.T, grads_row.reshape(count_py * local_y, wide), precision=precise
+    ).reshape(count_py, capacity * wide)
+    store_flat = lax.all_to_all(placed, "py", split_axis=0, concat_axis=0, tiled=True)
+    store_grad = jnp.transpose(
+        store_flat.reshape(channels, capacity, 2, channels), (1, 2, 0, 3)
+    )
     return (field_grad, store_grad)
 
 

time: 345 us -> 210 us (0.61)
  the two profiles are of different devices: /device:TPU:64 before, /device:TPU:1 now
where the time goes in v1:
time: 210 us; the launch traced here: 209 us
  blocking collectives  56.7 us (27%)
  waiting for transfers between devices  44.8 us (21%)
  starting transfers between devices  38.2 us (18%)
  local copies, waits for them, and re-layouts  31.4 us (15%)
  matrix products  26.7 us (13%)
  other arithmetic  10.3 us (5%)
    all_to_all x2, starting transfers between devices, inverse_planes(): lax.all_to_all(joined, 'px', split_axis=3, concat_axis=2, tiled=True)  22.8 us
    all_to_all x1, blocking collectives, on_device(): lax.all_to_all(jnp.concatenate([pieces_out, slots_out], 1), 'py', split_a...  19.1 us
    all_to_all x2, waiting for transfers between devices, inverse_planes(): lax.all_to_all(joined, 'px', split_axis=3, concat_axis=2, tiled=True)  17.1 us
    all_to_all x1, blocking collectives, on_device(): lax.all_to_all(partial_value, 'px', split_axis=2, concat_axis=3, tiled=True)  14.4 us
    unnamed x27, local copies, waits for them, and re-layouts  12.4 us
    all_to_all x1, blocking collectives, on_device(): lax.all_to_all(factor * jnp.stack([real_part, imag_part], -1), 'py', spli...  11.6 us
    all_to_all x1, blocking collectives, from_modes(): lax.all_to_all(spectrum, 'py', split_axis=1, concat_axis=3, tiled=True)  11.6 us
    dot_general x2, matrix products, inverse_planes(): jnp.einsum('czkx,yk->czxy', returned, table_y, precision=precise)  9.54 us
  transfers between devices with their start and end apart: 6, of which 6 were waited for; matrix products, arithmetic and copies ran while one was open for 6% of the time, Pallas kernels for 0%

profile of v1, /device:TPU:1, one launch (start us, length us, event | category | flops | bytes accessed | tf_op | source)
XLA Modules:
  0.0 209.4 jit_solution(6635024912092340591)
XLA Ops:
  2.7 19.1 %all_to_all.139 = f32[32,1,258]{2,1,0:T(1,128)S(1)} all-to-all(f32[32,1,258]{2,1,0:T(1,128)S(1)} %copy.147), channel_id=1, replica_groups=mesh['px'=16,'py'=32] {'py'}, dimensions={0} | all-to-all | bytes 66048 | tf_op jit(solution)/shard_map/all_to_all | solution.py:109
  22.9 3.8 %all-to-all-start.1 = ((f32[32,1,128]{2,1,0:T(1,128)}), f32[32,1,128]{2,1,0:T(1,128)S(1)}, u32[]{:S(2)}, u32[]{:S(2)}) async-start(f32[32,1,128]{2,1,0:T(1,128)} %bitcast.5), calls=%async_computation.1 | async-start | bytes 32768 | tf_op jit(solution)/shard_map/all_to_all | solution.py:118
  27.7 7.6 %all-to-all-done.1 = f32[32,1,128]{2,1,0:T(1,128)S(1)} async-done(((f32[32,1,128]{2,1,0:T(1,128)}), f32[32,1,128]{2,1,0:T(1,128)S(1)}, u32[]{:S(2)}, u32[]{:S(2)}) %all-to-all-start.1) | async-done | bytes 16416 | tf_op jit(solution)/shard_map/all_to_all | solution.py:118
  37.6 11.6 %all_to_all.140 = f32[32,1,128]{2,1,0:T(1,128)S(1)} all-to-all(f32[32,1,128]{2,1,0:T(1,128)S(1)} %reshape.417), channel_id=1, replica_groups=mesh['px'=16,'py'=32] {'py'}, dimensions={0} | all-to-all | bytes 32768 | tf_op jit(solution)/shard_map/all_to_all | solution.py:132
  54.8 14.7 %all-to-all-start.3 = ((f32[16,1,4096]{2,1,0:T(1,128)}), f32[16,1,4096]{2,1,0:T(1,128)S(1)}, u32[]{:S(2)}, u32[]{:S(2)}) async-start(f32[16,1,4096]{2,1,0:T(1,128)} %reshape.419), calls=%async_computation.3 | async-start | bytes 524288 | tf_op jit(solution)/shard_map/all_to_all | solution.py:122
  72.3 8.9 %all-to-all-done.3 = f32[16,1,4096]{2,1,0:T(1,128)S(1)} async-done(((f32[16,1,4096]{2,1,0:T(1,128)}), f32[16,1,4096]{2,1,0:T(1,128)S(1)}, u32[]{:S(2)}, u32[]{:S(2)}) %all-to-all-start.3) | async-done | bytes 262176 | tf_op jit(solution)/shard_map/all_to_all | solution.py:122
  84.7 6.6 %fusion.6 = f32[32,32,512]{2,0,1:T(8,128)S(1)} fusion(f32[32,32,512]{2,0,1:T(8,128)} %fusion.25, f32[32,64,32]{1,0,2:T(8,128)S(1)} %copy.187, f32[512,64,1]{0,1,2:T(8,128)S(1)} %reshape.396, bf16[32,1,32,512]{3,2,1,0:T(8,128)(2,1)} %param.10, f32[32]{0:T(128)S(1)} %copy-done.4), kind=kOutput, calls=%fused_computation.7 | convolution fusion | flops 409468928 | bytes 5636224 | tf_op jit(solution)/shard_map/czkx,yk->czxy/dot_general | solution.py:123
  92.7 2.6 %fusion.10 = f32[32,1,64,32]{2,3,0,1:T(8,128)S(1)} fusion(f32[512,64,1]{0,1,2:T(8,128)S(1)} %reshape.396, f32[32,32,512]{2,0,1:T(8,128)S(1)} %fusion.6), kind=kOutput, calls=%fused_computation.12 | convolution fusion | flops 402653184 | bytes 2490368 | tf_op jit(solution)/shard_map/czxy,yk->czkx/dot_general | solution.py:139
  96.7 14.4 %all_to_all.141 = f32[16,1,4096]{2,1,0:T(1,128)S(1)} all-to-all(f32[16,1,4096]{2,1,0:T(1,128)S(1)} %reshape.421), channel_id=1, replica_groups=mesh['px'=16,'py'=32] {'px'}, dimensions={0} | all-to-all | bytes 524288 | tf_op jit(solution)/shard_map/all_to_all | solution.py:140
  116.4 11.6 %all_to_all.142 = f32[32,1,128]{2,1,0:T(1,128)S(1)} all-to-all(f32[32,1,128]{2,1,0:T(1,128)S(1)} %reshape.423), channel_id=1, replica_groups=mesh['px'=16,'py'=32] {'py'}, dimensions={0} | all-to-all | bytes 32768 | tf_op jit(solution)/shard_map/all_to_all | solution.py:151
  131.3 3.8 %all-to-all-start.6 = ((f32[32,1,128]{2,1,0:T(1,128)}), f32[32,1,128]{2,1,0:T(1,128)S(1)}, u32[]{:S(2)}, u32[]{:S(2)}) async-start(f32[32,1,128]{2,1,0:T(1,128)} %reshape.425), calls=%async_computation.6 | async-start | bytes 32768 | tf_op jit(solution)/shard_map/all_to_all | solution.py:132
  135.9 7.8 %all-to-all-done.6 = f32[32,1,128]{2,1,0:T(1,128)S(1)} async-done(((f32[32,1,128]{2,1,0:T(1,128)}), f32[32,1,128]{2,1,0:T(1,128)S(1)}, u32[]{:S(2)}, u32[]{:S(2)}) %all-to-all-start.6) | async-done | bytes 16416 | tf_op jit(solution)/shard_map/all_to_all | solution.py:132
  143.7 3.9 %all-to-all-start.8 = ((f32[32,1,128]{2,1,0:T(1,128)}), f32[32,1,128]{2,1,0:T(1,128)S(1)}, u32[]{:S(2)}, u32[]{:S(2)}) async-start(f32[32,1,128]{2,1,0:T(1,128)} %bitcast.77), calls=%async_computation.8 | async-start | bytes 32768 | tf_op jit(solution)/shard_map/all_to_all | solution.py:164
  149.6 6.6 %all-to-all-done.8 = f32[32,1,128]{2,1,0:T(1,128)S(1)} async-done(((f32[32,1,128]{2,1,0:T(1,128)}), f32[32,1,128]{2,1,0:T(1,128)S(1)}, u32[]{:S(2)}, u32[]{:S(2)}) %all-to-all-start.8) | async-done | bytes 16416 | tf_op jit(solution)/shard_map/all_to_all | solution.py:164
  158.0 3.9 %all-to-all-start.9 = ((f32[32,1,256]{2,1,0:T(1,128)}), f32[32,1,256]{2,1,0:T(1,128)S(1)}, u32[]{:S(2)}, u32[]{:S(2)}) async-start(f32[32,1,256]{2,1,0:T(1,128)} %all_to_all.128), calls=%async_computation.9 | async-start | bytes 65536 | tf_op jit(solution)/shard_map/all_to_all | solution.py:168
  164.8 5.8 %all-to-all-done.9 = f32[32,1,256]{2,1,0:T(1,128)S(1)} async-done(((f32[32,1,256]{2,1,0:T(1,128)}), f32[32,1,256]{2,1,0:T(1,128)S(1)}, u32[]{:S(2)}, u32[]{:S(2)}) %all-to-all-start.9) | async-done | bytes 32800 | tf_op jit(solution)/shard_map/all_to_all | solution.py:168
  170.5 8.1 %all-to-all-start.7 = ((f32[16,1,4096]{2,1,0:T(1,128)}), f32[16,1,4096]{2,1,0:T(1,128)}, u32[]{:S(2)}, u32[]{:S(2)}) async-start(f32[16,1,4096]{2,1,0:T(1,128)} %reshape.427), calls=%async_computation.7 | async-start | bytes 524288 | tf_op jit(solution)/shard_map/all_to_all | solution.py:122
  178.6 2.9 %fusion.82 = f32[32,512,32]{1,2,0:T(8,128)S(1)} fusion(f32[32,32,512]{2,0,1:T(8,128)} %copy-done.1, bf16[32,32]{1,0:T(8,128)(2,1)S(1)} %copy-done.2), kind=kOutput, calls=%fused_computation.114 | convolution fusion | flops 201326592 | bytes 4196352 | tf_op jit(solution)/shard_map/oc,ozxy->czxy/dot_general | solution.py:160
  182.4 8.2 %all-to-all-done.7 = f32[16,1,4096]{2,1,0:T(1,128)} async-done(((f32[16,1,4096]{2,1,0:T(1,128)}), f32[16,1,4096]{2,1,0:T(1,128)}, u32[]{:S(2)}, u32[]{:S(2)}) %all-to-all-start.7) | async-done | bytes 262176 | tf_op jit(solution)/shard_map/all_to_all | solution.py:122
  190.6 3.0 %reduce.14 = f32[16,4096]{1,0:T(8,128)} reduce(f32[16,1,4096]{2,1,0:T(1,128)} %all-to-all-done.7, f32[]{:T(128)} %broadcast.245), dimensions={1}, to_apply=%all_to_all.121.reduce_sub_computation | reduce | bytes 524292 | tf_op jit(solution)/shard_map/all_to_all | solution.py:122
  196.0 2.6 %copy.200 = f32[32,1,4,16,32]{4,3,0,2,1:T(8,128)} copy(f32[32,1,4,16,32]{0,2,4,3,1:T(4,128)} %bitcast.239) | data formatting | bytes 524288 | tf_op jit(solution)/shard_map/all_to_all | solution.py:122
  201.2 2.7 %copy.190 = f32[32,64,32]{1,0,2:T(8,128)} copy(f32[32,64,32]{2,0,1:T(8,128)} %bitcast.243) | data formatting | bytes 524288 | tf_op jit(solution)/shard_map/reshape.74
  203.9 2.9 %fusion.7 = f32[32,1,32,512]{3,0,2,1:T(8,128)S(1)} fusion(f32[32,512,32]{1,2,0:T(8,128)S(1)} %fusion.82, f32[32,64,32]{1,0,2:T(8,128)} %copy.190, f32[512,64,1]{0,1,2:T(8,128)S(1)} %reshape.396), kind=kOutput, calls=%fused_computation.9 | convolution fusion | flops 403701760 | bytes 4587520 | tf_op jit(solution)/shard_map/czkx,yk->czxy/dot_general | solution.py:123
  206.8 2.5 %copy.185 = f32[32,1,32,512]{3,2,1,0:T(8,128)} copy(f32[32,1,32,512]{3,0,2,1:T(8,128)S(1)} %fusion.7) | data formatting | bytes 4194304
  (109 shorter events, 42.5 us)
Async XLA Ops:
  0.6 69.5 %copy-start = (bf16[32,1,32,512]{3,2,1,0:T(8,128)(2,1)S(1)}, bf16[32,1,32,512]{3,2,1,0:T(8,128)(2,1)}, u32[]{:S(2)}) copy-start(bf16[32,1,32,512]{3,2,1,0:T(8,128)(2,1)} %param.9) | copy-start | bytes 3145732
  0.6 50.1 %copy-start.5 = (s32[32]{0:T(128)S(1)}, s32[32]{0:T(128)}, u32[]{:S(2)}) copy-start(s32[32]{0:T(128)} %param.14) | copy-start | bytes 388
  22.9 12.4 %all-to-all-start.1 = ((f32[32,1,128]{2,1,0:T(1,128)}), f32[32,1,128]{2,1,0:T(1,128)S(1)}, u32[]{:S(2)}, u32[]{:S(2)}) async-start(f32[32,1,128]{2,1,0:T(1,128)} %bitcast.5), calls=%async_computation.1 | async-start | bytes 32768 | tf_op jit(solution)/shard_map/all_to_all | solution.py:118
  53.0 16.5 %copy-start.3 = (s32[32]{0:T(128)S(1)}, s32[32]{0:T(128)}, u32[]{:S(2)}) copy-start(s32[32]{0:T(128)} %param.15) | copy-start | bytes 388
  53.0 17.1 %copy-start.2 = (bf16[32,32]{1,0:T(8,128)(2,1)S(1)}, bf16[32,32]{1,0:T(8,128)(2,1)}, u32[]{:S(2)}) copy-start(bf16[32,32]{1,0:T(8,128)(2,1)} %param.16) | copy-start | bytes 6148
  54.8 26.4 %all-to-all-start.3 = ((f32[16,1,4096]{2,1,0:T(1,128)}), f32[16,1,4096]{2,1,0:T(1,128)S(1)}, u32[]{:S(2)}, u32[]{:S(2)}) async-start(f32[16,1,4096]{2,1,0:T(1,128)} %reshape.419), calls=%async_computation.3 | async-start | bytes 524288 | tf_op jit(solution)/shard_map/all_to_all | solution.py:122
  83.6 1.1 copy-start.4
  91.3 1.3 copy-start.1
  131.3 12.4 %all-to-all-start.6 = ((f32[32,1,128]{2,1,0:T(1,128)}), f32[32,1,128]{2,1,0:T(1,128)S(1)}, u32[]{:S(2)}, u32[]{:S(2)}) async-start(f32[32,1,128]{2,1,0:T(1,128)} %reshape.425), calls=%async_computation.6 | async-start | bytes 32768 | tf_op jit(solution)/shard_map/all_to_all | solution.py:132
  143.7 12.5 %all-to-all-start.8 = ((f32[32,1,128]{2,1,0:T(1,128)}), f32[32,1,128]{2,1,0:T(1,128)S(1)}, u32[]{:S(2)}, u32[]{:S(2)}) async-start(f32[32,1,128]{2,1,0:T(1,128)} %bitcast.77), calls=%async_computation.8 | async-start | bytes 32768 | tf_op jit(solution)/shard_map/all_to_all | solution.py:164
  158.0 12.6 %all-to-all-start.9 = ((f32[32,1,256]{2,1,0:T(1,128)}), f32[32,1,256]{2,1,0:T(1,128)S(1)}, u32[]{:S(2)}, u32[]{:S(2)}) async-start(f32[32,1,256]{2,1,0:T(1,128)} %all_to_all.128), calls=%async_computation.9 | async-start | bytes 65536 | tf_op jit(solution)/shard_map/all_to_all | solution.py:168
  170.5 20.1 %all-to-all-start.7 = ((f32[16,1,4096]{2,1,0:T(1,128)}), f32[16,1,4096]{2,1,0:T(1,128)}, u32[]{:S(2)}, u32[]{:S(2)}) async-start(f32[16,1,4096]{2,1,0:T(1,128)} %reshape.427), calls=%async_computation.7 | async-start | bytes 524288 | tf_op jit(solution)/shard_map/all_to_all | solution.py:122

commit v2 on v0

v2 whole, which is shorter than its diff:
```python
import functools
import math

import jax
import jax.numpy as jnp
from jax import lax
from jax.experimental import pallas as pl
from jax.experimental.pallas import tpu as pltpu
from jax.sharding import PartitionSpec as P

MESH = pl.DeviceIdType.MESH
HIGH = lax.Precision.HIGH
EXACT = lax.Precision.HIGHEST
NN = (((1,), (0,)), ((), ()))
NT = (((1,), (1,)), ((), ()))
TN = (((0,), (0,)), ((), ()))


def dot(a, b, dims, precision=HIGH):
    return lax.dot_general(
        a, b, dims, precision=precision, preferred_element_type=jnp.float32
    )


def gelu_slope(values):
    normal_cdf = 0.5 * (1.0 + lax.erf(values * 0.7071067811865476))
    density = jnp.exp(-0.5 * values * values) * 0.3989422804014327
    return normal_cdf + values * density


def iota(shape, axis):
    return lax.broadcasted_iota(jnp.int32, shape, axis)


def spread_map(pointwise, group, dims):
    channels = pointwise.shape[0]
    size = channels * group
    left = (iota((size, channels), 0) // group == iota((size, channels), 1)).astype(jnp.bfloat16)
    right = (iota((channels, size), 1) // group == iota((channels, size), 0)).astype(jnp.bfloat16)
    half = lax.dot_general(left, pointwise, dims, preferred_element_type=jnp.float32)
    full = jnp.dot(half.astype(jnp.bfloat16), right, preferred_element_type=jnp.float32)
    same = (iota((size, size), 0) & (group - 1)) == (iota((size, size), 1) & (group - 1))
    return jnp.where(same, full, 0.0).astype(jnp.bfloat16)


def turned(values, imag):
    return jnp.where(imag, pltpu.roll(values, 32, 1), -pltpu.roll(values, 96, 1))


def kernel(
    n_px,
    n_py,
    field_hbm,
    cot_hbm,
    saved_ref,
    store_ref,
    slots_ref,
    table_x_ref,
    table_y_ref,
    pointwise_ref,
    bias_ref,
    out_hbm,
    store_out_ref,
    field_ref,
    cot_ref,
    pre_ref,
    grad_ref,
    rows_ref,
    back_ref,
    piece_out,
    piece_in,
    chosen_out,
    chosen_in,
    mixed_out,
    mixed_in,
    plane_out,
    plane_in,
    part_out,
    part_in,
    whole_out,
    whole_in,
    adj_out,
    adj_in,
    last_out,
    last_in,
    block_out,
    block_in,
    slot_out,
    slot_in,
    send_sem,
    recv_sem,
    local_sem,
):
    mine_x = lax.axis_index("px")
    mine_y = lax.axis_index("py")
    channels = 32
    groups = channels // 4

    def send(phase, src, dst, axis, whole=False):
        n, me = (n_px, mine_x) if axis == "px" else (n_py, mine_y)

        def one(step, carry):
            peer = lax.rem(me + step, n)
            pltpu.make_async_remote_copy(
                src_ref=src if whole else src.at[peer],
                dst_ref=dst.at[me],
                send_sem=send_sem.at[phase],
                recv_sem=recv_sem.at[phase],
                device_id={axis: peer},
                device_id_type=MESH,
            ).start()
            return carry

        lax.fori_loop(1, n, one, 0)
        dst[me] = src[...] if whole else src[me]

    def bulk(phase, dst, axis):
        n, me = (n_px, mine_x) if axis == "px" else (n_py, mine_y)
        span = dst.at[pl.ds(0, n - 1)]
        return pltpu.make_async_remote_copy(
            src_ref=span,
            dst_ref=span,
            send_sem=send_sem.at[phase],
            recv_sem=recv_sem.at[phase],
            device_id={axis: lax.rem(me + 1, n)},
            device_id_type=MESH,
        )

    field_copy = pltpu.make_async_copy(field_hbm, field_ref, local_sem.at[0])
    cot_copy = pltpu.make_async_copy(cot_hbm, cot_ref, local_sem.at[1])
    field_copy.start()
    cot_copy.start()

    barrier = pltpu.get_barrier_semaphore()

    def greet(axis):
        n, me = (n_px, mine_x) if axis == "px" else (n_py, mine_y)

        def one(step, carry):
            pl.semaphore_signal(
                barrier, inc=1, device_id={axis: lax.rem(me + step, n)}, device_id_type=MESH
            )
            return carry

        lax.fori_loop(1, n, one, 0)

    greet("py")
    greet("px")

    wide = jnp.concatenate([store_ref[k] for k in range(8)], axis=1)
    piece_out[:, 0, 0:256] = wide
    piece_out[:, 0, 256:384] = jnp.broadcast_to(slots_ref[...], (n_py, 128))
    pl.semaphore_wait(barrier, n_px + n_py - 2)
    send(0, piece_out, piece_in, "py")

    pointwise = pointwise_ref[...]
    forward_map = spread_map(pointwise, 16, NN)
    backward_map = spread_map(pointwise, 8, NT)
    field_copy.wait()
    for part in range(2):
        cut = pl.ds(16 * part, 16)
        block = field_ref[:, cut, :].reshape(16 * channels, 512)
        mapped = jnp.dot(forward_map, block, preferred_element_type=jnp.float32)
        pre_ref[:, cut, :] = mapped.reshape(channels, 16, 512)

    lane = iota((1, 128), 1)
    imag = (lane & 32) != 0
    first = lane < 64
    slot_of_lane = ((lane & 31) * 4 + (lane >> 5)).astype(jnp.float32)

    bulk(0, piece_in, "py").wait_recv()
    pieces = jnp.concatenate([piece_in[:, 0, 64 * s : 64 * s + 64] for s in range(4)], axis=0)
    slots = piece_in[:, 0, 256:384]
    selects = [
        jnp.where(slots[:, b : b + 1] == slot_of_lane, 1.0, 0.0).astype(jnp.float32)
        for b in range(2)
    ]
    chosen_out[:, 0, :] = jnp.concatenate(
        [dot(select, pieces, NN, EXACT) for select in selects], axis=1
    )
    send(1, chosen_out, chosen_in, "py")

    saved = saved_ref[...]
    table_x = table_x_ref[...]
    table_y = table_y_ref[...]

    bulk(1, chosen_in, "py").wait_recv()
    weights = chosen_in[:, 0, :]
    signed = jnp.where(imag, -weights, weights)
    swapped = jnp.where(imag, pltpu.roll(weights, 32, 1), pltpu.roll(weights, 96, 1))
    mix = jnp.concatenate(
        [
            jnp.where(first, signed, 0.0),
            jnp.where(first, swapped, 0.0),
            jnp.where(first, 0.0, signed),
            jnp.where(first, 0.0, swapped),
        ],
        axis=0,
    )
    mixed_out[:, 0, :] = dot(saved, mix, NT)
    send(2, mixed_out, mixed_in, "py")

    bulk(2, mixed_in, "py").wait_recv()
    plane_out[...] = mixed_in[:, 0, :]
    send(3, plane_out, plane_in, "px", whole=True)

    def to_rows(planes):
        def one(p, carry):
            plane = planes[p]
            both = jnp.concatenate([plane, turned(plane, imag)], axis=0)
            rows_ref[pl.ds(pl.multiple_of(p * 128, 128), 128), :] = dot(both, table_x, TN)
            return carry

        lax.fori_loop(0, n_px, one, 0)

    lane_group = lane >> 5

    def row_block(i):
        picked = rows_ref[pl.ds(4 * i, 64, stride=32), :]
        for g in range(1, 4):
            picked = jnp.where(
                lane_group == g, rows_ref[pl.ds(4 * i + g, 64, stride=32), :], picked
            )
        return dot(picked, table_y, TN)

    cot_copy.wait()
    bulk(3, plane_in, "px").wait_recv()
    to_rows(plane_in)

    def grad_block(i, carry):
        spectral = row_block(i)
        parts = []
        for g in range(4):
            o = 4 * i + g
            pre = pre_ref[o] + bias_ref[o] + spectral[32 * g : 32 * g + 32]
            grad = cot_ref[o].astype(jnp.float32) * gelu_slope(pre)
            grad_ref[o] = grad
            parts.append(grad)
        freq = dot(table_y, jnp.concatenate(parts, axis=0), NT)
        for g in range(4):
            back_ref[pl.ds(4 * i + g, 64, stride=32), :] = freq
        return carry

    lax.fori_loop(0, groups, grad_block, 0)

    own_group = (iota((128, 128), 0) & 3) == (iota((128, 128), 1) >> 5)

    def part_block(p, carry):
        rows = back_ref[pl.ds(pl.multiple_of(p * 128, 128), 128), :]
        both = dot(table_x, jnp.where(own_group, rows, 0.0), NT)
        part_out[p] = both[0:32] - turned(both[32:64], imag)
        return carry

    lax.fori_loop(0, n_px, part_block, 0)
    send(4, part_out, part_in, "px")

    for part in range(4):
        cut = pl.ds(8 * part, 8)
        block = grad_ref[:, cut, :].reshape(8 * channels, 512)
        upper = block.astype(jnp.bfloat16)
        lower = (block - upper.astype(jnp.float32)).astype(jnp.bfloat16)
        base = jnp.dot(backward_map, upper, preferred_element_type=jnp.float32) + jnp.dot(
            backward_map, lower, preferred_element_type=jnp.float32
        )
        pre_ref[:, cut, :] = base.reshape(channels, 8, 512)

    bulk(4, part_in, "px").wait_recv()
    total = part_in[0]
    for p in range(1, n_px):
        total = total + part_in[p]
    whole_out[:, 0, :] = total
    send(5, whole_out, whole_in, "py")

    bulk(5, whole_in, "py").wait_recv()
    spectrum_grad = whole_in[:, 0, :]
    adj_out[:, 0, :] = dot(spectrum_grad, mix, NN)
    send(6, adj_out, adj_in, "py")

    cross = dot(spectrum_grad, saved, TN)
    blocks = None
    for b in range(2):
        re = cross[64 * b : 64 * b + 32]
        im = cross[64 * b + 32 : 64 * b + 64]
        value = jnp.where(
            imag, im_shift(im, 32) - re, re + im_shift(im, 96)
        )
        blocks = value if b == 0 else jnp.where(first, blocks, value)
    block_out[:, 0, :] = blocks
    send(7, block_out, block_in, "py")

    bulk(6, adj_in, "py").wait_recv()
    last_out[...] = adj_in[:, 0, :]
    send(8, last_out, last_in, "px", whole=True)

    bulk(7, block_in, "py").wait_recv()
    received = block_in[:, 0, :]
    placed = dot(selects[0], received[:, 0:64], TN, EXACT) + dot(
        selects[1], received[:, 64:128], TN, EXACT
    )
    slot_out[:, 0, :] = jnp.concatenate([placed[32 * s : 32 * s + 32] for s in range(4)], axis=1)
    send(9, slot_out, slot_in, "py")

    bulk(8, last_in, "px").wait_recv()
    to_rows(last_in)

    def out_copy(i):
        cut = pl.ds(4 * i, 4)
        return pltpu.make_async_copy(pre_ref.at[cut], out_hbm.at[cut], local_sem.at[2])

    def out_block(i, carry):
        spectral = row_block(i)
        for g in range(4):
            o = 4 * i + g
            pre_ref[o] = pre_ref[o] + spectral[32 * g : 32 * g + 32]
        return carry

    lax.fori_loop(0, groups, out_block, 0)
    final = pltpu.make_async_copy(pre_ref, out_hbm, local_sem.at[2])
    final.start()

    bulk(9, slot_in, "py").wait_recv()
    for k in range(8):
        store_out_ref[k] = slot_in[:, 0, 32 * k : 32 * k + 32]
    final.wait()
    for phase, dst, axis in (
        (0, piece_in, "py"),
        (1, chosen_in, "py"),
        (2, mixed_in, "py"),
        (3, plane_in, "px"),
        (4, part_in, "px"),
        (5, whole_in, "py"),
        (6, adj_in, "py"),
        (7, block_in, "py"),
        (8, last_in, "px"),
        (9, slot_in, "py"),
    ):
        bulk(phase, dst, axis).wait_send()


def im_shift(values, amount):
    return pltpu.roll(values, amount, 1)


def on_device(
    n_px,
    n_py,
    field_in,
    cotangent,
    spectrum_saved,
    weight_store,
    block_slot,
    kx_modes,
    ky_modes,
    pointwise,
    bias_vector,
):
    channels, _, rows_x, width_y = field_in.shape
    full_x = rows_x * n_px
    factor = 1.0 / math.sqrt(full_x * width_y)
    points_y = lax.iota(jnp.int32, width_y)
    angle_y = (points_y[None, :] * ky_modes[:, None] % width_y).astype(jnp.float32) * (
        2.0 * math.pi / width_y
    )
    table_y = jnp.stack([jnp.cos(angle_y), -jnp.sin(angle_y)], 1).reshape(-1, width_y)
    points_x = lax.axis_index("px") * rows_x + (lax.iota(jnp.int32, 4 * rows_x) % rows_x)
    angle_x = (points_x[None, :] * kx_modes[:, None] % full_x).astype(jnp.float32) * (
        2.0 * math.pi / full_x
    )
    table_x = factor * jnp.concatenate([jnp.cos(angle_x), jnp.sin(angle_x)], 0)
    saved = jnp.transpose(spectrum_saved[:, :, :, 0, :], (1, 2, 3, 0)).reshape(n_py, 4 * channels)
    slots = jnp.pad(block_slot.astype(jnp.float32), ((0, 0), (0, 126)))
    vmem = pl.BlockSpec(memory_space=pltpu.VMEM)
    hbm = pl.BlockSpec(memory_space=pl.ANY)
    f32 = jnp.float32
    row = pltpu.VMEM((n_py, 1, 128), f32)
    tile = pltpu.VMEM((32, 128), f32)
    tiles = pltpu.VMEM((n_px, 32, 128), f32)
    field_grad, store_grad = pl.pallas_call(
        functools.partial(kernel, n_px, n_py),
        out_shape=(
            jax.ShapeDtypeStruct((channels, rows_x, width_y), f32),
            jax.ShapeDtypeStruct((8, channels, channels), f32),
        ),
        in_specs=[hbm, hbm, vmem, vmem, vmem, vmem, vmem, vmem]
        + [pl.BlockSpec(memory_space=pltpu.SMEM)],
        out_specs=(hbm, vmem),
        scratch_shapes=[
            pltpu.VMEM((channels, rows_x, width_y), jnp.bfloat16),
            pltpu.VMEM((channels, rows_x, width_y), jnp.bfloat16),
            pltpu.VMEM((channels, rows_x, width_y), f32),
            pltpu.VMEM((channels, rows_x, width_y), f32),
            pltpu.VMEM((n_px * 128, 128), f32),
            pltpu.VMEM((n_px * 128, 128), f32),
            pltpu.VMEM((n_py, 1, 384), f32),
            pltpu.VMEM((n_py, 1, 384), f32),
            row,
            row,
            row,
            row,
            tile,
            tiles,
            tiles,
            tiles,
            row,
            row,
            row,
            row,
            tile,
            tiles,
            row,
            row,
            pltpu.VMEM((n_py, 1, 256), f32),
            pltpu.VMEM((n_py, 1, 256), f32),
            pltpu.SemaphoreType.DMA((10,)),
            pltpu.SemaphoreType.DMA((10,)),
            pltpu.SemaphoreType.DMA((3,)),
        ],
        compiler_params=pltpu.CompilerParams(
            collective_id=0, has_side_effects=True, vmem_limit_bytes=48 << 20
        ),
    )(
        field_in.reshape(channels, rows_x, width_y),
        cotangent.reshape(channels, rows_x, width_y),
        saved,
        weight_store.reshape(8, channels, channels),
        slots,
        table_x,
        table_y,
        pointwise,
        bias_vector,
    )
    return (
        field_grad.reshape(field_in.shape),
        store_grad.reshape(weight_store.shape),
    )


def solution(mesh):
    placed = (
        P(None, "py", "px", None),
        P(None, "py", "px", None),
        P(None, None, "px", "py", None),
        P(("px", "py"), None, None, None),
        P("py", "px"),
        P(),
        P(),
        P(),
        P(),
    )
    return jax.shard_map(
        functools.partial(on_device, mesh.shape["px"], mesh.shape["py"]),
        mesh=mesh,
        in_specs=placed,
        out_specs=(P(None, "py", "px", None), P(("px", "py"), None, None, None)),
        check_vma=False,
    )
```

time: 345 us -> 103 us (0.30)
  the two profiles are of different devices: /device:TPU:64 before, /device:TPU:1 now
where the time goes in v2:
time: 103 us
  Pallas kernels  91.7 us (89%)
  local copies, waits for them, and re-layouts  7.93 us (8%)
  other arithmetic  2.48 us (2%)
    pallas_call x1, Pallas kernels, on_device(): pl.pallas_call(functools.partial(kernel, n_px, n_py), out_shape=(jax.Shap...  91.7 us
    unnamed x12, local copies, waits for them, and re-layouts  6.68 us

profile of v2, /device:TPU:1, one launch (start us, length us, event | category | flops | bytes accessed | tf_op | source)
XLA Modules:
  0.0 102.8 jit_solution(14026003232170830163)
XLA Ops:
  0.6 0.7 convert_element_type.22
  1.3 0.8 fusion.11
  2.1 0.9 copy.13
  3.1 0.1 reshape.132.saved_ref
  3.2 1.0 fusion.6
  4.2 0.1 copy.14
  4.3 0.1 reshape.134.table_y_ref
  4.4 0.0 copy-start
  4.4 1.2 %copy-done = bf16[32,1,32,512]{3,2,1,0:T(8,128)(2,1)S(1)} copy-done((bf16[32,1,32,512]{3,2,1,0:T(8,128)(2,1)S(1)}, bf16[32,1,32,512]{3,2,1,0:T(8,128)(2,1)}, u32[]{:S(2)}) %copy-start) | copy-done | bytes 1048600
  5.7 0.0 copy-start.1
  5.7 1.2 %copy-done.1 = bf16[32,1,32,512]{3,2,1,0:T(8,128)(2,1)S(1)} copy-done((bf16[32,1,32,512]{3,2,1,0:T(8,128)(2,1)S(1)}, bf16[32,1,32,512]{3,2,1,0:T(8,128)(2,1)}, u32[]{:S(2)}) %copy-start.1) | copy-done | bytes 1048600
  6.9 0.0 copy-start.2
  6.9 0.9 copy-done.2
  7.8 0.0 copy-start.3
  7.8 0.7 copy-done.3
  8.5 0.0 copy-start.4
  8.5 0.7 copy-done.4
  9.1 91.7 %shard_map.104 = (f32[32,32,512]{2,1,0:T(8,128)S(1)}, f32[8,32,32]{2,1,0:T(8,128)S(1)}) custom-call(bf16[32,32,512]{2,1,0:T(8,128)(2,1)S(1)} %bitcast.11, bf16[32,32,512]{2,1,0:T(8,128)(2,1)S(1)} %bitcast.12, f32[32,128]{1,0:T(8,128)S(1)} %reshape.132.saved_ref, f32[8,32,32]{2,1,0:T(8,128)S(1)} %bitcast.13, f32[1,128]{1,0:T(1,128)S(1)} %pad.4.slots_ref, ...), custom_call_target="tpu_custom_call" | custom-call | tf_op jit(solution)/shard_map/pallas_call | solution.py:378
  100.9 1.3 %copy.18 = f32[32,1,32,512]{3,2,1,0:T(8,128)} copy(f32[32,1,32,512]{3,2,1,0:T(8,128)S(1)} %bitcast.10) | data formatting | bytes 4194304
  102.2 0.7 copy.19
  (4 shorter events, 0.0 us)
Async XLA Ops:
  4.4 1.2 %copy-start = (bf16[32,1,32,512]{3,2,1,0:T(8,128)(2,1)S(1)}, bf16[32,1,32,512]{3,2,1,0:T(8,128)(2,1)}, u32[]{:S(2)}) copy-start(bf16[32,1,32,512]{3,2,1,0:T(8,128)(2,1)} %param.9) | copy-start | bytes 3145732
  5.7 1.2 %copy-start.1 = (bf16[32,1,32,512]{3,2,1,0:T(8,128)(2,1)S(1)}, bf16[32,1,32,512]{3,2,1,0:T(8,128)(2,1)}, u32[]{:S(2)}) copy-start(bf16[32,1,32,512]{3,2,1,0:T(8,128)(2,1)} %param.10) | copy-start | bytes 3145732
  6.9 0.9 copy-start.2
  7.8 0.7 copy-start.3
  8.5 0.7 copy-start.4

commit v3 on v2

--- a/solution.py
+++ b/solution.py
@@ -14,6 +14,8 @@
 NN = (((1,), (0,)), ((), ()))
 NT = (((1,), (1,)), ((), ()))
 TN = (((0,), (0,)), ((), ()))
+STEPS = (1, 7, 2, 6, 3, 5, 4)
+BATCHES = ((1, 7, 2, 6), (3, 5, 4))
 
 
 def dot(a, b, dims, precision=HIGH):
@@ -43,6 +45,17 @@
     return jnp.where(same, full, 0.0).astype(jnp.bfloat16)
 
 
+def column(row_ref, size, repeat):
+    count = row_ref.shape[1]
+    same = iota((size, count), 0) // repeat == iota((size, count), 1)
+    row = row_ref[...].astype(jnp.float32)
+    return jnp.sum(jnp.where(same, row, 0.0), axis=1, keepdims=True).astype(jnp.int32)
+
+
+def angle(points, length):
+    return (points & (length - 1)).astype(jnp.float32) * (2.0 * math.pi / length)
+
+
 def turned(values, imag):
     return jnp.where(imag, pltpu.roll(values, 32, 1), -pltpu.roll(values, 96, 1))
 
@@ -52,17 +65,26 @@
     n_py,
     field_hbm,
     cot_hbm,
+    saved_hbm,
+    store_hbm,
+    slots_hbm,
+    kx_hbm,
+    ky_hbm,
+    pointwise_hbm,
+    bias_hbm,
+    out_hbm,
+    store_out_hbm,
+    field_ref,
+    cot_ref,
     saved_ref,
     store_ref,
     slots_ref,
-    table_x_ref,
-    table_y_ref,
+    kx_ref,
+    ky_ref,
     pointwise_ref,
     bias_ref,
-    out_hbm,
+    table_y_ref,
     store_out_ref,
-    field_ref,
-    cot_ref,
     pre_ref,
     grad_ref,
     rows_ref,
@@ -77,6 +99,7 @@
     plane_in,
     part_out,
     part_in,
+    half_in,
     whole_out,
     whole_in,
     adj_out,
@@ -89,10 +112,15 @@
     slot_in,
     send_sem,
     recv_sem,
+    px_sem,
+    part_sem,
     local_sem,
 ):
     mine_x = lax.axis_index("px")
     mine_y = lax.axis_index("py")
+    sibling = mine_x + 1 - 2 * lax.rem(mine_x, 2)
+    full_x = 32 * n_px
+    factor = 1.0 / math.sqrt(full_x * 512)
     channels = 32
     groups = channels // 4
 
@@ -126,12 +154,29 @@
             device_id_type=MESH,
         )
 
-    field_copy = pltpu.make_async_copy(field_hbm, field_ref, local_sem.at[0])
-    cot_copy = pltpu.make_async_copy(cot_hbm, cot_ref, local_sem.at[1])
-    field_copy.start()
-    cot_copy.start()
+    loads = [
+        pltpu.make_async_copy(src, dst, local_sem.at[k])
+        for k, (src, dst) in enumerate(
+            (
+                (store_hbm, store_ref),
+                (slots_hbm, slots_ref),
+                (kx_hbm, kx_ref),
+                (ky_hbm, ky_ref),
+                (pointwise_hbm, pointwise_ref),
+                (bias_hbm, bias_ref),
+                (saved_hbm, saved_ref),
+                (field_hbm, field_ref),
+                (cot_hbm, cot_ref),
+            )
+        )
+    ]
+    for load in loads:
+        load.start()
 
     barrier = pltpu.get_barrier_semaphore()
+
+    def signal_px(peer):
+        pl.semaphore_signal(barrier, inc=1, device_id={"px": peer}, device_id_type=MESH)
 
     def greet(axis):
         n, me = (n_px, mine_x) if axis == "px" else (n_py, mine_y)
@@ -145,22 +190,30 @@
         lax.fori_loop(1, n, one, 0)
 
     greet("py")
-    greet("px")
-
+    for step in STEPS:
+        signal_px(lax.rem(mine_x + 2 * step, n_px))
+    signal_px(sibling)
+
+    loads[0].wait()
+    loads[1].wait()
     wide = jnp.concatenate([store_ref[k] for k in range(8)], axis=1)
     piece_out[:, 0, 0:256] = wide
-    piece_out[:, 0, 256:384] = jnp.broadcast_to(slots_ref[...], (n_py, 128))
-    pl.semaphore_wait(barrier, n_px + n_py - 2)
+    piece_out[:, 0, 256:384] = jnp.zeros((n_py, 128), jnp.float32)
+    piece_out[:, 0, 256:258] = jnp.broadcast_to(slots_ref[...].astype(jnp.float32), (n_py, 2))
+    pl.semaphore_wait(barrier, n_py + len(STEPS))
     send(0, piece_out, piece_in, "py")
 
+    for load in loads[2:8]:
+        load.wait()
     pointwise = pointwise_ref[...]
     forward_map = spread_map(pointwise, 16, NN)
     backward_map = spread_map(pointwise, 8, NT)
-    field_copy.wait()
+    owner = iota((16 * channels, channels), 0) // 16 == iota((16 * channels, channels), 1)
+    bias = jnp.sum(jnp.where(owner, bias_ref[...], 0.0), axis=1, keepdims=True)
     for part in range(2):
         cut = pl.ds(16 * part, 16)
         block = field_ref[:, cut, :].reshape(16 * channels, 512)
-        mapped = jnp.dot(forward_map, block, preferred_element_type=jnp.float32)
+        mapped = jnp.dot(forward_map, block, preferred_element_type=jnp.float32) + bias
         pre_ref[:, cut, :] = mapped.reshape(channels, 16, 512)
 
     lane = iota((1, 128), 1)
@@ -180,8 +233,16 @@
     )
     send(1, chosen_out, chosen_in, "py")
 
-    saved = saved_ref[...]
-    table_x = table_x_ref[...]
+    saved = jnp.concatenate(
+        [saved_ref[:, b, r, :] for b in range(2) for r in range(2)], axis=0
+    ).T
+    kx = column(kx_ref, 32, 1)
+    angle_x = angle((mine_x * 32 + (iota((32, 128), 1) & 31)) * kx, full_x)
+    table_x = jnp.concatenate([jnp.cos(angle_x), jnp.sin(angle_x)], axis=0) * factor
+    ky = column(ky_ref, 64, 2)
+    angle_y = angle(iota((64, 512), 1) * ky, 512)
+    even = (iota((64, 512), 0) & 1) == 0
+    table_y_ref[...] = jnp.where(even, jnp.cos(angle_y), -jnp.sin(angle_y))
     table_y = table_y_ref[...]
 
     bulk(1, chosen_in, "py").wait_recv()
@@ -200,18 +261,58 @@
     mixed_out[:, 0, :] = dot(saved, mix, NT)
     send(2, mixed_out, mixed_in, "py")
 
+    def px_copy(k, src, dst, source, peer):
+        return pltpu.make_async_remote_copy(
+            src_ref=src,
+            dst_ref=dst,
+            send_sem=send_sem.at[(3, 4, 8)[k]],
+            recv_sem=px_sem.at[k, source],
+            device_id={"px": peer},
+            device_id_type=MESH,
+        )
+
+    def to_rows(planes, sources):
+        both = jnp.concatenate(
+            [
+                jnp.concatenate([planes[p], turned(planes[p], imag)], axis=0)
+                for p in sources
+            ],
+            axis=1,
+        )
+        rows = dot(both, table_x, TN)
+        for n, p in enumerate(sources):
+            rows_ref[pl.ds(pl.multiple_of(p * 128, 128), 128), :] = rows[
+                128 * n : 128 * n + 128
+            ]
+
+    def scatter_plane(k, src, dst):
+        px_copy(k, src, dst.at[mine_x], mine_x, sibling).start()
+        for step in STEPS:
+            peer = lax.rem(mine_x + 2 * step, n_px)
+            px_copy(k, src, dst.at[mine_x], mine_x, peer).start()
+        dst[mine_x] = src[...]
+
+    def collect_planes(k, dst):
+        def arrived(p):
+            px_copy(k, dst.at[p], dst.at[p], p, sibling).wait_recv()
+
+        arrived(sibling)
+        to_rows(dst, [mine_x, sibling])
+        for batch in BATCHES:
+            sources = [lax.rem(mine_x + n_px - 2 * step, n_px) for step in batch]
+            for p in sources:
+                arrived(p)
+                px_copy(k, dst.at[p], dst.at[p], p, sibling).start()
+            to_rows(dst, sources)
+        for batch in BATCHES:
+            sources = [lax.rem(sibling + n_px - 2 * step, n_px) for step in batch]
+            for p in sources:
+                arrived(p)
+            to_rows(dst, sources)
+
     bulk(2, mixed_in, "py").wait_recv()
     plane_out[...] = mixed_in[:, 0, :]
-    send(3, plane_out, plane_in, "px", whole=True)
-
-    def to_rows(planes):
-        def one(p, carry):
-            plane = planes[p]
-            both = jnp.concatenate([plane, turned(plane, imag)], axis=0)
-            rows_ref[pl.ds(pl.multiple_of(p * 128, 128), 128), :] = dot(both, table_x, TN)
-            return carry
-
-        lax.fori_loop(0, n_px, one, 0)
+    scatter_plane(0, plane_out, plane_in)
 
     lane_group = lane >> 5
 
@@ -223,16 +324,15 @@
             )
         return dot(picked, table_y, TN)
 
-    cot_copy.wait()
-    bulk(3, plane_in, "px").wait_recv()
-    to_rows(plane_in)
+    loads[8].wait()
+    collect_planes(0, plane_in)
 
     def grad_block(i, carry):
         spectral = row_block(i)
         parts = []
         for g in range(4):
             o = 4 * i + g
-            pre = pre_ref[o] + bias_ref[o] + spectral[32 * g : 32 * g + 32]
+            pre = pre_ref[o] + spectral[32 * g : 32 * g + 32]
             grad = cot_ref[o].astype(jnp.float32) * gelu_slope(pre)
             grad_ref[o] = grad
             parts.append(grad)
@@ -245,14 +345,43 @@
 
     own_group = (iota((128, 128), 0) & 3) == (iota((128, 128), 1) >> 5)
 
-    def part_block(p, carry):
-        rows = back_ref[pl.ds(pl.multiple_of(p * 128, 128), 128), :]
-        both = dot(table_x, jnp.where(own_group, rows, 0.0), NT)
-        part_out[p] = both[0:32] - turned(both[32:64], imag)
-        return carry
-
-    lax.fori_loop(0, n_px, part_block, 0)
-    send(4, part_out, part_in, "px")
+    def part_tiles(targets):
+        rows = jnp.concatenate(
+            [
+                jnp.where(
+                    own_group, back_ref[pl.ds(pl.multiple_of(p * 128, 128), 128), :], 0.0
+                )
+                for p in targets
+            ],
+            axis=0,
+        )
+        both = dot(table_x, rows, NT)
+        tiles = [both[:, 128 * n : 128 * n + 128] for n in range(len(targets))]
+        return [tile[0:32] - turned(tile[32:64], imag) for tile in tiles]
+
+    for batch in (STEPS[0:4], STEPS[4:] + (0,)):
+        targets = [lax.rem(sibling + 2 * step, n_px) for step in batch]
+        for p, tile in zip(targets, part_tiles(targets)):
+            part_out[p] = tile
+            px_copy(1, part_out.at[p], half_in.at[p], p, sibling).start()
+    total = None
+    for batch in (STEPS[0:4], STEPS[4:] + (0,)):
+        targets = [lax.rem(mine_x + 2 * step, n_px) for step in batch]
+        for step, p, tile in zip(batch, targets, part_tiles(targets)):
+            px_copy(1, half_in.at[p], half_in.at[p], p, sibling).wait_recv()
+            tile = tile + half_in[p]
+            if step == 0:
+                total = tile
+            else:
+                part_out[p] = tile
+                pltpu.make_async_remote_copy(
+                    src_ref=part_out.at[p],
+                    dst_ref=part_in.at[mine_x],
+                    send_sem=send_sem.at[4],
+                    recv_sem=part_sem.at[mine_x],
+                    device_id={"px": p},
+                    device_id_type=MESH,
+                ).start()
 
     for part in range(4):
         cut = pl.ds(8 * part, 8)
@@ -264,9 +393,16 @@
         )
         pre_ref[:, cut, :] = base.reshape(channels, 8, 512)
 
-    bulk(4, part_in, "px").wait_recv()
-    total = part_in[0]
-    for p in range(1, n_px):
+    for step in STEPS:
+        p = lax.rem(mine_x + n_px - 2 * step, n_px)
+        pltpu.make_async_remote_copy(
+            src_ref=part_in.at[p],
+            dst_ref=part_in.at[p],
+            send_sem=send_sem.at[4],
+            recv_sem=part_sem.at[p],
+            device_id={"px": sibling},
+            device_id_type=MESH,
+        ).wait_recv()
         total = total + part_in[p]
     whole_out[:, 0, :] = total
     send(5, whole_out, whole_in, "py")
@@ -290,7 +426,7 @@
 
     bulk(6, adj_in, "py").wait_recv()
     last_out[...] = adj_in[:, 0, :]
-    send(8, last_out, last_in, "px", whole=True)
+    scatter_plane(2, last_out, last_in)
 
     bulk(7, block_in, "py").wait_recv()
     received = block_in[:, 0, :]
@@ -300,28 +436,27 @@
     slot_out[:, 0, :] = jnp.concatenate([placed[32 * s : 32 * s + 32] for s in range(4)], axis=1)
     send(9, slot_out, slot_in, "py")
 
-    bulk(8, last_in, "px").wait_recv()
-    to_rows(last_in)
-
-    def out_copy(i):
-        cut = pl.ds(4 * i, 4)
-        return pltpu.make_async_copy(pre_ref.at[cut], out_hbm.at[cut], local_sem.at[2])
+    collect_planes(2, last_in)
 
     def out_block(i, carry):
         spectral = row_block(i)
         for g in range(4):
             o = 4 * i + g
             pre_ref[o] = pre_ref[o] + spectral[32 * g : 32 * g + 32]
+        cut = pl.ds(4 * i, 4)
+        pltpu.make_async_copy(pre_ref.at[cut], out_hbm.at[cut], local_sem.at[9]).start()
         return carry
 
     lax.fori_loop(0, groups, out_block, 0)
-    final = pltpu.make_async_copy(pre_ref, out_hbm, local_sem.at[2])
-    final.start()
+    final = pltpu.make_async_copy(pre_ref, out_hbm, local_sem.at[9])
 
     bulk(9, slot_in, "py").wait_recv()
     for k in range(8):
         store_out_ref[k] = slot_in[:, 0, 32 * k : 32 * k + 32]
+    last = pltpu.make_async_copy(store_out_ref, store_out_hbm, local_sem.at[10])
+    last.start()
     final.wait()
+    last.wait()
     for phase, dst, axis in (
         (0, piece_in, "py"),
         (1, chosen_in, "py"),
@@ -355,22 +490,7 @@
     bias_vector,
 ):
     channels, _, rows_x, width_y = field_in.shape
-    full_x = rows_x * n_px
-    factor = 1.0 / math.sqrt(full_x * width_y)
-    points_y = lax.iota(jnp.int32, width_y)
-    angle_y = (points_y[None, :] * ky_modes[:, None] % width_y).astype(jnp.float32) * (
-        2.0 * math.pi / width_y
-    )
-    table_y = jnp.stack([jnp.cos(angle_y), -jnp.sin(angle_y)], 1).reshape(-1, width_y)
-    points_x = lax.axis_index("px") * rows_x + (lax.iota(jnp.int32, 4 * rows_x) % rows_x)
-    angle_x = (points_x[None, :] * kx_modes[:, None] % full_x).astype(jnp.float32) * (
-        2.0 * math.pi / full_x
-    )
-    table_x = factor * jnp.concatenate([jnp.cos(angle_x), jnp.sin(angle_x)], 0)
-    saved = jnp.transpose(spectrum_saved[:, :, :, 0, :], (1, 2, 3, 0)).reshape(n_py, 4 * channels)
-    slots = jnp.pad(block_slot.astype(jnp.float32), ((0, 0), (0, 126)))
-    vmem = pl.BlockSpec(memory_space=pltpu.VMEM)
-    hbm = pl.BlockSpec(memory_space=pl.ANY)
+    hbm = pl.BlockSpec(memory_space=pltpu.HBM)
     f32 = jnp.float32
     row = pltpu.VMEM((n_py, 1, 128), f32)
     tile = pltpu.VMEM((32, 128), f32)
@@ -381,12 +501,20 @@
             jax.ShapeDtypeStruct((channels, rows_x, width_y), f32),
             jax.ShapeDtypeStruct((8, channels, channels), f32),
         ),
-        in_specs=[hbm, hbm, vmem, vmem, vmem, vmem, vmem, vmem]
-        + [pl.BlockSpec(memory_space=pltpu.SMEM)],
-        out_specs=(hbm, vmem),
+        in_specs=[hbm] * 9,
+        out_specs=(hbm, hbm),
         scratch_shapes=[
             pltpu.VMEM((channels, rows_x, width_y), jnp.bfloat16),
             pltpu.VMEM((channels, rows_x, width_y), jnp.bfloat16),
+            pltpu.VMEM((channels, 2, 2, n_py), f32),
+            pltpu.VMEM((8, channels, channels), f32),
+            pltpu.VMEM((1, 2), jnp.int32),
+            pltpu.VMEM((1, 32), jnp.int32),
+            pltpu.VMEM((1, 32), jnp.int32),
+            pltpu.VMEM((channels, channels), jnp.bfloat16),
+            pltpu.VMEM((1, channels), f32),
+            pltpu.VMEM((64, width_y), f32),
+            pltpu.VMEM((8, channels, channels), f32),
             pltpu.VMEM((channels, rows_x, width_y), f32),
             pltpu.VMEM((channels, rows_x, width_y), f32),
             pltpu.VMEM((n_px * 128, 128), f32),
@@ -401,6 +529,7 @@
             tiles,
             tiles,
             tiles,
+            tiles,
             row,
             row,
             row,
@@ -413,21 +542,23 @@
             pltpu.VMEM((n_py, 1, 256), f32),
             pltpu.SemaphoreType.DMA((10,)),
             pltpu.SemaphoreType.DMA((10,)),
-            pltpu.SemaphoreType.DMA((3,)),
+            pltpu.SemaphoreType.DMA((3, n_px)),
+            pltpu.SemaphoreType.DMA((n_px,)),
+            pltpu.SemaphoreType.DMA((11,)),
         ],
         compiler_params=pltpu.CompilerParams(
-            collective_id=0, has_side_effects=True, vmem_limit_bytes=48 << 20
+            collective_id=0, has_side_effects=True, vmem_limit_bytes=63 << 20
         ),
     )(
         field_in.reshape(channels, rows_x, width_y),
         cotangent.reshape(channels, rows_x, width_y),
-        saved,
+        jnp.transpose(spectrum_saved[:, :, :, 0, :], (0, 2, 3, 1)),
         weight_store.reshape(8, channels, channels),
-        slots,
-        table_x,
-        table_y,
+        block_slot,
+        kx_modes.reshape(1, -1),
+        ky_modes.reshape(1, -1),
         pointwise,
-        bias_vector,
+        bias_vector.reshape(1, -1),
     )
     return (
         field_grad.reshape(field_in.shape),

time: 103 us -> 83.7 us (0.81)
  Pallas kernels: 91.7 us -> 79 us
  local copies, waits for them, and re-layouts: 7.93 us -> 3.88 us
  other arithmetic: 2.48 us -> 0 us
    pallas_call x1, Pallas kernels: 91.7 us -> 79 us  [on_device(): pl.pallas_call(functools.partial(kernel, n_px, n_py), out_shape=(jax.Shap...]
    unnamed x12 -> x4, local copies, waits for them, and re-layouts: 6.68 us -> 3.88 us
    cos x2 -> x0, other arithmetic: 1.8 us -> none  [the longest x1 1 us: on_device(): jnp.cos(angle_y)]
where the time goes in v3:
time: 83.7 us; the launch traced here: 83.5 us
  Pallas kernels  79 us (94%)
  local copies, waits for them, and re-layouts  3.88 us (5%)
    pallas_call x1, Pallas kernels, on_device(): pl.pallas_call(functools.partial(kernel, n_px, n_py), out_shape=(jax.Shap...  79 us
    unnamed x4, local copies, waits for them, and re-layouts  3.88 us

profile of v3, /device:TPU:1, one launch (start us, length us, event | category | flops | bytes accessed | tf_op | source)
XLA Modules:
  0.0 83.5 jit_solution(9498262538346439178)
XLA Ops:
  0.6 79.0 %shard_map.104 = (f32[32,32,512]{2,1,0:T(8,128)}, f32[8,32,32]{2,1,0:T(8,128)}) custom-call(bf16[32,32,512]{2,1,0:T(8,128)(2,1)} %bitcast.14, bf16[32,32,512]{2,1,0:T(8,128)(2,1)} %bitcast.15, f32[32,2,2,32]{3,2,1,0:T(2,128)} %bitcast.18, f32[8,32,32]{2,1,0:T(8,128)} %bitcast.17, s32[1,2]{1,0:T(1,128)} %slots_hbm.1, s32[1,32]{1,0:T(1,128)} %bitcast.19, ...), custom_call_target="tpu_custom_call" | custom-call | tf_op jit(solution)/shard_map/pallas_call | solution.py:498
  79.6 0.0 copy-start
  79.7 3.2 %copy.14 = f32[32,1,32,512]{3,2,1,0:T(8,128)} copy(f32[32,1,32,512]{3,2,1,0:T(8,128)} %bitcast.13) | data formatting | bytes 4194304
  82.9 0.0 copy-done
  82.9 0.7 copy.15
Async XLA Ops:
  79.6 3.2 %copy-start = (f32[8,32,32]{2,1,0:T(8,128)S(1)}, f32[8,32,32]{2,1,0:T(8,128)}, u32[]{:S(2)}) copy-start(f32[8,32,32]{2,1,0:T(8,128)} %get-tuple-element.5) | copy-start | bytes 98308

commit v4 on v3

--- a/solution.py
+++ b/solution.py
@@ -72,8 +72,8 @@
     ky_hbm,
     pointwise_hbm,
     bias_hbm,
-    out_hbm,
-    store_out_hbm,
+    out_ref,
+    store_out_ref,
     field_ref,
     cot_ref,
     saved_ref,
@@ -84,7 +84,6 @@
     pointwise_ref,
     bias_ref,
     table_y_ref,
-    store_out_ref,
     pre_ref,
     grad_ref,
     rows_ref,
@@ -102,8 +101,8 @@
     half_in,
     whole_out,
     whole_in,
-    adj_out,
-    adj_in,
+    wall_out,
+    wall_in,
     last_out,
     last_in,
     block_out,
@@ -228,9 +227,9 @@
         jnp.where(slots[:, b : b + 1] == slot_of_lane, 1.0, 0.0).astype(jnp.float32)
         for b in range(2)
     ]
-    chosen_out[:, 0, :] = jnp.concatenate(
-        [dot(select, pieces, NN, EXACT) for select in selects], axis=1
-    )
+    chosen = jnp.concatenate([dot(select, pieces, NN, EXACT) for select in selects], axis=1)
+    chosen_out[:, 0, :] = chosen
+    wall_out[...] = chosen
     send(1, chosen_out, chosen_in, "py")
 
     saved = jnp.concatenate(
@@ -260,6 +259,7 @@
     )
     mixed_out[:, 0, :] = dot(saved, mix, NT)
     send(2, mixed_out, mixed_in, "py")
+    send(6, wall_out, wall_in, "py", whole=True)
 
     def px_copy(k, src, dst, source, peer):
         return pltpu.make_async_remote_copy(
@@ -341,7 +341,7 @@
             back_ref[pl.ds(4 * i + g, 64, stride=32), :] = freq
         return carry
 
-    lax.fori_loop(0, groups, grad_block, 0)
+    lax.fori_loop(0, groups, grad_block, 0, unroll=2)
 
     own_group = (iota((128, 128), 0) & 3) == (iota((128, 128), 1) >> 5)
 
@@ -407,11 +407,21 @@
     whole_out[:, 0, :] = total
     send(5, whole_out, whole_in, "py")
 
+    bulk(6, wall_in, "py").wait_recv()
+    by_re = by_im = None
+    for o in range(channels):
+        wall = wall_in[o]
+        re = wall * jnp.where(first, total[:, o : o + 1], total[:, 64 + o : 65 + o])
+        im = wall * jnp.where(first, total[:, 32 + o : 33 + o], total[:, 96 + o : 97 + o])
+        by_re = re if o == 0 else by_re + re
+        by_im = im if o == 0 else by_im + im
+    last_out[...] = jnp.where(
+        imag, pltpu.roll(by_im, 32, 1) - by_re, by_re + pltpu.roll(by_im, 96, 1)
+    )
+    scatter_plane(2, last_out, last_in)
+
     bulk(5, whole_in, "py").wait_recv()
     spectrum_grad = whole_in[:, 0, :]
-    adj_out[:, 0, :] = dot(spectrum_grad, mix, NN)
-    send(6, adj_out, adj_in, "py")
-
     cross = dot(spectrum_grad, saved, TN)
     blocks = None
     for b in range(2):
@@ -424,9 +434,16 @@
     block_out[:, 0, :] = blocks
     send(7, block_out, block_in, "py")
 
-    bulk(6, adj_in, "py").wait_recv()
-    last_out[...] = adj_in[:, 0, :]
-    scatter_plane(2, last_out, last_in)
+    collect_planes(2, last_in)
+
+    def out_block(i, carry):
+        spectral = row_block(i)
+        for g in range(4):
+            o = 4 * i + g
+            out_ref[o] = pre_ref[o] + spectral[32 * g : 32 * g + 32]
+        return carry
+
+    lax.fori_loop(0, groups // 2, out_block, 0, unroll=2)
 
     bulk(7, block_in, "py").wait_recv()
     received = block_in[:, 0, :]
@@ -436,27 +453,11 @@
     slot_out[:, 0, :] = jnp.concatenate([placed[32 * s : 32 * s + 32] for s in range(4)], axis=1)
     send(9, slot_out, slot_in, "py")
 
-    collect_planes(2, last_in)
-
-    def out_block(i, carry):
-        spectral = row_block(i)
-        for g in range(4):
-            o = 4 * i + g
-            pre_ref[o] = pre_ref[o] + spectral[32 * g : 32 * g + 32]
-        cut = pl.ds(4 * i, 4)
-        pltpu.make_async_copy(pre_ref.at[cut], out_hbm.at[cut], local_sem.at[9]).start()
-        return carry
-
-    lax.fori_loop(0, groups, out_block, 0)
-    final = pltpu.make_async_copy(pre_ref, out_hbm, local_sem.at[9])
+    lax.fori_loop(groups // 2, groups, out_block, 0, unroll=2)
 
     bulk(9, slot_in, "py").wait_recv()
     for k in range(8):
         store_out_ref[k] = slot_in[:, 0, 32 * k : 32 * k + 32]
-    last = pltpu.make_async_copy(store_out_ref, store_out_hbm, local_sem.at[10])
-    last.start()
-    final.wait()
-    last.wait()
     for phase, dst, axis in (
         (0, piece_in, "py"),
         (1, chosen_in, "py"),
@@ -464,7 +465,7 @@
         (3, plane_in, "px"),
         (4, part_in, "px"),
         (5, whole_in, "py"),
-        (6, adj_in, "py"),
+        (6, wall_in, "py"),
         (7, block_in, "py"),
         (8, last_in, "px"),
         (9, slot_in, "py"),
@@ -498,11 +499,11 @@
     field_grad, store_grad = pl.pallas_call(
         functools.partial(kernel, n_px, n_py),
         out_shape=(
-            jax.ShapeDtypeStruct((channels, rows_x, width_y), f32),
-            jax.ShapeDtypeStruct((8, channels, channels), f32),
+            pltpu.VMEM((channels, rows_x, width_y), f32),
+            pltpu.VMEM((8, channels, channels), f32),
         ),
         in_specs=[hbm] * 9,
-        out_specs=(hbm, hbm),
+        out_specs=(pl.BlockSpec(memory_space=pltpu.VMEM),) * 2,
         scratch_shapes=[
             pltpu.VMEM((channels, rows_x, width_y), jnp.bfloat16),
             pltpu.VMEM((channels, rows_x, width_y), jnp.bfloat16),
@@ -514,7 +515,6 @@
             pltpu.VMEM((channels, channels), jnp.bfloat16),
             pltpu.VMEM((1, channels), f32),
             pltpu.VMEM((64, width_y), f32),
-            pltpu.VMEM((8, channels, channels), f32),
             pltpu.VMEM((channels, rows_x, width_y), f32),
             pltpu.VMEM((channels, rows_x, width_y), f32),
             pltpu.VMEM((n_px * 128, 128), f32),
@@ -532,8 +532,8 @@
             tiles,
             row,
             row,
-            row,
-            row,
+            tile,
+            pltpu.VMEM((n_py, 32, 128), f32),
             tile,
             tiles,
             row,
@@ -544,12 +544,13 @@
             pltpu.SemaphoreType.DMA((10,)),
             pltpu.SemaphoreType.DMA((3, n_px)),
             pltpu.SemaphoreType.DMA((n_px,)),
-            pltpu.SemaphoreType.DMA((11,)),
+            pltpu.SemaphoreType.DMA((9,)),
         ],
         compiler_params=pltpu.CompilerParams(
-            collective_id=0, has_side_effects=True, vmem_limit_bytes=63 << 20
+            collective_id=0, has_side_effects=True, vmem_limit_bytes=48 << 20
         ),
     )(
+        *held(
         field_in.reshape(channels, rows_x, width_y),
         cotangent.reshape(channels, rows_x, width_y),
         jnp.transpose(spectrum_saved[:, :, :, 0, :], (0, 2, 3, 1)),
@@ -559,11 +560,16 @@
         ky_modes.reshape(1, -1),
         pointwise,
         bias_vector.reshape(1, -1),
+            )
     )
     return (
         field_grad.reshape(field_in.shape),
         store_grad.reshape(weight_store.shape),
     )
+
+
+def held(*arrays):
+    return [pltpu.with_memory_space_constraint(array, pltpu.HBM) for array in arrays]
 
 
 def solution(mesh):

time: 83.7 us -> 73.8 us (0.88)
  Pallas kernels: 79 us -> 71 us
  local copies, waits for them, and re-layouts: 3.88 us -> 1.98 us
    pallas_call x1, Pallas kernels: 79 us -> 71 us  [on_device(): pl.pallas_call(functools.partial(kernel, n_px, n_py), out_shape=(pltpu.VM...]
    unnamed x4 -> x2, local copies, waits for them, and re-layouts: 3.88 us -> 1.98 us
where the time goes in v4:
time: 73.8 us; the launch traced here: 73.6 us
  Pallas kernels  71 us (96%)
  local copies, waits for them, and re-layouts  1.98 us (3%)
    pallas_call x1, Pallas kernels, on_device(): pl.pallas_call(functools.partial(kernel, n_px, n_py), out_shape=(pltpu.VM...  71 us
    unnamed x2, local copies, waits for them, and re-layouts  1.98 us

profile of v4, /device:TPU:1, one launch (start us, length us, event | category | flops | bytes accessed | tf_op | source)
XLA Modules:
  0.0 73.6 jit_solution(6908298076093032190)
XLA Ops:
  0.6 71.0 %shard_map.104 = (f32[32,32,512]{2,1,0:T(8,128)S(1)}, f32[8,32,32]{2,1,0:T(8,128)S(1)}) custom-call(bf16[32,32,512]{2,1,0:T(8,128)(2,1)} %bitcast.15, bf16[32,32,512]{2,1,0:T(8,128)(2,1)} %bitcast.16, f32[32,2,2,32]{3,2,1,0:T(2,128)} %bitcast.18, f32[8,32,32]{2,1,0:T(8,128)} %bitcast.17, s32[1,2]{1,0:T(1,128)} %slots_hbm.1, s32[1,32]{1,0:T(1,128)} %bitcast.19, ...), custom_call_target="tpu_custom_call" | custom-call | tf_op jit(solution)/shard_map/pallas_call | solution.py:499
  71.6 1.3 %copy.14 = f32[32,1,32,512]{3,2,1,0:T(8,128)} copy(f32[32,1,32,512]{3,2,1,0:T(8,128)S(1)} %bitcast.13) | data formatting | bytes 4194304
  73.0 0.7 copy.15

commit v5 on v4

--- a/solution.py
+++ b/solution.py
@@ -105,8 +105,9 @@
     wall_in,
     last_out,
     last_in,
-    block_out,
-    block_in,
+    saved_out,
+    saved_in,
+    sums_ref,
     slot_out,
     slot_in,
     send_sem,
@@ -235,6 +236,7 @@
     saved = jnp.concatenate(
         [saved_ref[:, b, r, :] for b in range(2) for r in range(2)], axis=0
     ).T
+    saved_out[...] = saved
     kx = column(kx_ref, 32, 1)
     angle_x = angle((mine_x * 32 + (iota((32, 128), 1) & 31)) * kx, full_x)
     table_x = jnp.concatenate([jnp.cos(angle_x), jnp.sin(angle_x)], axis=0) * factor
@@ -313,6 +315,7 @@
     bulk(2, mixed_in, "py").wait_recv()
     plane_out[...] = mixed_in[:, 0, :]
     scatter_plane(0, plane_out, plane_in)
+    send(7, saved_out, saved_in, "py", whole=True)
 
     lane_group = lane >> 5
 
@@ -404,35 +407,53 @@
             device_id_type=MESH,
         ).wait_recv()
         total = total + part_in[p]
-    whole_out[:, 0, :] = total
+    turned_total = total.T
+    whole_out[:, 0, :] = jnp.concatenate(
+        [turned_total[32 * k : 32 * k + 32] for k in range(4)], axis=1
+    )
     send(5, whole_out, whole_in, "py")
 
+    def pair(rows, k):
+        return jnp.where(first, rows[:, k : k + 1], rows[:, 64 + k : 65 + k])
+
+    def crossed(by_re, by_im):
+        return jnp.where(
+            imag, pltpu.roll(by_im, 32, 1) - by_re, by_re + pltpu.roll(by_im, 96, 1)
+        )
+
     bulk(6, wall_in, "py").wait_recv()
-    by_re = by_im = None
-    for o in range(channels):
+    def wall_step(o, carry):
+        rows, by_re, by_im = carry
         wall = wall_in[o]
-        re = wall * jnp.where(first, total[:, o : o + 1], total[:, 64 + o : 65 + o])
-        im = wall * jnp.where(first, total[:, 32 + o : 33 + o], total[:, 96 + o : 97 + o])
-        by_re = re if o == 0 else by_re + re
-        by_im = im if o == 0 else by_im + im
-    last_out[...] = jnp.where(
-        imag, pltpu.roll(by_im, 32, 1) - by_re, by_re + pltpu.roll(by_im, 96, 1)
-    )
+        return (
+            pltpu.roll(rows, 127, 1),
+            by_re + wall * pair(rows, 0),
+            by_im + wall * pair(rows, 32),
+        )
+
+    zero = jnp.zeros((32, 128), jnp.float32)
+    _, by_re, by_im = lax.fori_loop(0, channels, wall_step, (total, zero, zero), unroll=4)
+    last_out[...] = crossed(by_re, by_im)
     scatter_plane(2, last_out, last_in)
 
     bulk(5, whole_in, "py").wait_recv()
-    spectrum_grad = whole_in[:, 0, :]
-    cross = dot(spectrum_grad, saved, TN)
-    blocks = None
-    for b in range(2):
-        re = cross[64 * b : 64 * b + 32]
-        im = cross[64 * b + 32 : 64 * b + 64]
-        value = jnp.where(
-            imag, im_shift(im, 32) - re, re + im_shift(im, 96)
-        )
-        blocks = value if b == 0 else jnp.where(first, blocks, value)
-    block_out[:, 0, :] = blocks
-    send(7, block_out, block_in, "py")
+    bulk(7, saved_in, "py").wait_recv()
+    grads = whole_in[:, 0, :]
+
+    def saved_step(k, grads):
+        inputs = saved_in[k]
+        for part in range(2):
+            sums = jnp.sum(inputs * pair(grads, 32 * part), axis=0, keepdims=True)
+            sums_ref[part, pl.ds(k, 1), :] = sums
+        return pltpu.roll(grads, 127, 1)
+
+    lax.fori_loop(0, 32, saved_step, grads, unroll=4)
+    received = crossed(sums_ref[0], sums_ref[1])
+    placed = dot(selects[0], received[:, 0:64], TN, EXACT) + dot(
+        selects[1], received[:, 64:128], TN, EXACT
+    )
+    slot_out[:, 0, :] = jnp.concatenate([placed[32 * s : 32 * s + 32] for s in range(4)], axis=1)
+    send(9, slot_out, slot_in, "py")
 
     collect_planes(2, last_in)
 
@@ -443,17 +464,7 @@
             out_ref[o] = pre_ref[o] + spectral[32 * g : 32 * g + 32]
         return carry
 
-    lax.fori_loop(0, groups // 2, out_block, 0, unroll=2)
-
-    bulk(7, block_in, "py").wait_recv()
-    received = block_in[:, 0, :]
-    placed = dot(selects[0], received[:, 0:64], TN, EXACT) + dot(
-        selects[1], received[:, 64:128], TN, EXACT
-    )
-    slot_out[:, 0, :] = jnp.concatenate([placed[32 * s : 32 * s + 32] for s in range(4)], axis=1)
-    send(9, slot_out, slot_in, "py")
-
-    lax.fori_loop(groups // 2, groups, out_block, 0, unroll=2)
+    lax.fori_loop(0, groups, out_block, 0, unroll=2)
 
     bulk(9, slot_in, "py").wait_recv()
     for k in range(8):
@@ -466,15 +477,11 @@
         (4, part_in, "px"),
         (5, whole_in, "py"),
         (6, wall_in, "py"),
-        (7, block_in, "py"),
+        (7, saved_in, "py"),
         (8, last_in, "px"),
         (9, slot_in, "py"),
     ):
         bulk(phase, dst, axis).wait_send()
-
-
-def im_shift(values, amount):
-    return pltpu.roll(values, amount, 1)
 
 
 def on_device(
@@ -536,8 +543,9 @@
             pltpu.VMEM((n_py, 32, 128), f32),
             tile,
             tiles,
-            row,
-            row,
+            tile,
+            pltpu.VMEM((n_py, 32, 128), f32),
+            pltpu.VMEM((2, 32, 128), f32),
             pltpu.VMEM((n_py, 1, 256), f32),
             pltpu.VMEM((n_py, 1, 256), f32),
             pltpu.SemaphoreType.DMA((10,)),

time: 73.8 us -> 71 us (0.962)
  Pallas kernels: 71 us -> 68.3 us
    pallas_call x1, Pallas kernels: 71 us -> 68.3 us  [on_device(): pl.pallas_call(functools.partial(kernel, n_px, n_py), out_shape=(pltpu.VM...]
where the time goes in v5:
time: 71 us; the launch traced here: 70.9 us
  Pallas kernels  68.3 us (96%)
  local copies, waits for them, and re-layouts  1.98 us (3%)
    pallas_call x1, Pallas kernels, on_device(): pl.pallas_call(functools.partial(kernel, n_px, n_py), out_shape=(pltpu.VM...  68.3 us
    unnamed x2, local copies, waits for them, and re-layouts  1.98 us

profile of v5, /device:TPU:1, one launch (start us, length us, event | category | flops | bytes accessed | tf_op | source)
XLA Modules:
  0.0 70.9 jit_solution(7208657056281356400)
XLA Ops:
  0.6 68.3 %shard_map.104 = (f32[32,32,512]{2,1,0:T(8,128)S(1)}, f32[8,32,32]{2,1,0:T(8,128)S(1)}) custom-call(bf16[32,32,512]{2,1,0:T(8,128)(2,1)} %bitcast.15, bf16[32,32,512]{2,1,0:T(8,128)(2,1)} %bitcast.16, f32[32,2,2,32]{3,2,1,0:T(2,128)} %bitcast.18, f32[8,32,32]{2,1,0:T(8,128)} %bitcast.17, s32[1,2]{1,0:T(1,128)} %slots_hbm.1, s32[1,32]{1,0:T(1,128)} %bitcast.19, ...), custom_call_target="tpu_custom_call" | custom-call | tf_op jit(solution)/shard_map/pallas_call | solution.py:506
  68.9 1.3 %copy.14 = f32[32,1,32,512]{3,2,1,0:T(8,128)} copy(f32[32,1,32,512]{3,2,1,0:T(8,128)S(1)} %bitcast.13) | data formatting | bytes 4194304
  70.2 0.7 copy.15

commit v6 on v5

--- a/solution.py
+++ b/solution.py
@@ -344,7 +344,7 @@
             back_ref[pl.ds(4 * i + g, 64, stride=32), :] = freq
         return carry
 
-    lax.fori_loop(0, groups, grad_block, 0, unroll=2)
+    lax.fori_loop(0, groups, grad_block, 0, unroll=4)
 
     own_group = (iota((128, 128), 0) & 3) == (iota((128, 128), 1) >> 5)
 
@@ -464,7 +464,7 @@
             out_ref[o] = pre_ref[o] + spectral[32 * g : 32 * g + 32]
         return carry
 
-    lax.fori_loop(0, groups, out_block, 0, unroll=2)
+    lax.fori_loop(0, groups, out_block, 0, unroll=4)
 
     bulk(9, slot_in, "py").wait_recv()
     for k in range(8):

time: 71 us -> 70.2 us (0.989)
  Pallas kernels: 68.3 us -> 67 us
    pallas_call x1, Pallas kernels: 68.3 us -> 67 us  [on_device(): pl.pallas_call(functools.partial(kernel, n_px, n_py), out_shape=(pltpu.VM...]
where the time goes in v6:
time: 70.2 us; the launch traced here: 69.6 us
  Pallas kernels  67 us (95%)
  local copies, waits for them, and re-layouts  1.98 us (3%)
    pallas_call x1, Pallas kernels, on_device(): pl.pallas_call(functools.partial(kernel, n_px, n_py), out_shape=(pltpu.VM...  67 us
    unnamed x2, local copies, waits for them, and re-layouts  1.98 us

profile of v6, /device:TPU:1, one launch (start us, length us, event | category | flops | bytes accessed | tf_op | source)
XLA Modules:
  0.0 69.6 jit_solution(10848748464935169554)
XLA Ops:
  0.6 67.0 %shard_map.104 = (f32[32,32,512]{2,1,0:T(8,128)S(1)}, f32[8,32,32]{2,1,0:T(8,128)S(1)}) custom-call(bf16[32,32,512]{2,1,0:T(8,128)(2,1)} %bitcast.15, bf16[32,32,512]{2,1,0:T(8,128)(2,1)} %bitcast.16, f32[32,2,2,32]{3,2,1,0:T(2,128)} %bitcast.18, f32[8,32,32]{2,1,0:T(8,128)} %bitcast.17, s32[1,2]{1,0:T(1,128)} %slots_hbm.1, s32[1,32]{1,0:T(1,128)} %bitcast.19, ...), custom_call_target="tpu_custom_call" | custom-call | tf_op jit(solution)/shard_map/pallas_call | solution.py:506
  67.6 1.3 %copy.14 = f32[32,1,32,512]{3,2,1,0:T(8,128)} copy(f32[32,1,32,512]{3,2,1,0:T(8,128)S(1)} %bitcast.13) | data formatting | bytes 4194304
  68.9 0.7 copy.15
